TPU v7x, 256 devices: a whole 4x4x8 slice. The times are simulated.
256 devices in a mesh: pipe: 8 (over y, core), expert: 32 (over x, z).
Axes of the slice: x: 4, y: 4, z: 8, core: 2. Of those that a mesh axis runs over, the one named last changes fastest.
Arguments:
- saved_inputs: bfloat16 [8, 4096, 2048], P('pipe', 'expert'), may hold values from -6 to 6
- grad_out: bfloat16 [8, 4096, 2048], P('pipe', 'expert'), may hold values from -6 to 6
- routes: int32 [8, 4096, 8], P('pipe', 'expert'), may hold values from 0 to 31, all different within a row; in each aligned block of 128 rows (0 to 127, 128 to 255, ..., all dimensions but the last counted through in order) at most 36 rows name the same one
- route_probs: float32 [8, 4096, 8], P('pipe', 'expert'), may hold values from 0.1 to 0.6
- w_in: bfloat16 [8, 32, 2048, 768], P('pipe', 'expert'), may hold values from -0.125 to 0.125
- w_out: bfloat16 [8, 32, 384, 2048], P('pipe', 'expert'), may hold values from -0.3125 to 0.3125
Outputs:
- grad_tokens: float32 [8, 4096, 2048], P('pipe', 'expert')
- grad_w_in: bfloat16 [8, 32, 2048, 768], P('pipe', 'expert')
- grad_w_out: bfloat16 [8, 32, 384, 2048], P('pipe', 'expert')
Inputs may be any that keep to these rules, and one draw needn't show every extreme that they name: `routes`: each row names 8 different experts. Among the rows of one device (aligned blocks of 128 rows) no expert is named more than 36 times, a bound that some block reaches.
All inputs are finite; a program needn't handle non-finite values.
Results may differ from a plain program's by a relative error of at most 0.0057.
Values may be sent and summed in bfloat16 or wider, within the bound.
No kernel may reach another device: no remote copies, remote signals or barrier semaphores. Data moves between devices by JAX's collectives and lax.ppermute only.
A program may use at most 128 MiB of HBM per device.

v0:
```python
import functools
import jax
import jax.numpy as jnp
from jax import lax
from jax.experimental import pallas as pl
from jax.experimental.pallas import tpu as pltpu
from jax.sharding import PartitionSpec as P

CAP = 36
XN = 4
ZN = 8
TOK = 128
TILE = 512
HALF = 256
F32 = jnp.float32
BF16 = jnp.bfloat16
VMEM_LIMIT = 16 * 1024 * 1024
VMEM = pl.BlockSpec(memory_space=pltpu.VMEM)
NT = (((1,), (1,)), ((), ()))
TN = (((0,), (0,)), ((), ()))


def round_up(value, unit):
    return -(-value // unit) * unit


def shaped(rows, width, kind=BF16):
    return jax.ShapeDtypeStruct((rows, width), kind)


def run(kernel, outs, args, flops, moved, scratch=(), smem=0):
    specs = [pl.BlockSpec(memory_space=pltpu.SMEM)] * smem + [VMEM] * (len(args) - smem)
    return pl.pallas_call(
        kernel,
        out_shape=outs,
        in_specs=specs,
        out_specs=[VMEM] * len(outs),
        scratch_shapes=scratch,
        compiler_params=pltpu.CompilerParams(vmem_limit_bytes=VMEM_LIMIT),
        cost_estimate=pl.CostEstimate(flops=flops, bytes_accessed=moved, transcendentals=0),
    )(*args)


def each_tile(count, size, step):
    def body(i, carry):
        step(pl.multiple_of(i * size, size))
        return carry

    lax.fori_loop(0, count, body, 0)


def select_rows(ids_ref, meta, slot, sel_ref):
    total = meta.shape[1]
    ids = meta[0:8]
    probs = meta[8:16] + meta[16:24] + meta[24:32]
    marks, weights = [], []
    for j in range(XN):
        hit = ids == ids_ref[0, j].astype(F32)
        marks.append(jnp.sum(jnp.where(hit, 1.0, 0.0), axis=0, keepdims=True))
        weights.append(jnp.sum(jnp.where(hit, probs, 0.0), axis=0, keepdims=True))
    mark = jnp.concatenate(marks + [jnp.zeros((8 - XN, total), F32)], axis=0)
    earlier = lax.broadcasted_iota(jnp.int32, (total, total), 0) < lax.broadcasted_iota(
        jnp.int32, (total, total), 1
    )
    rank = jnp.dot(
        mark.astype(BF16), jnp.where(earlier, 1.0, 0.0).astype(BF16), preferred_element_type=F32
    )
    place = lax.broadcasted_iota(jnp.int32, (slot, total), 0).astype(F32)
    scales = []
    for j in range(XN):
        wanted = jnp.where(mark[j : j + 1] > 0.5, rank[j : j + 1], -1.0)
        chosen = place == wanted
        sel_ref[j * slot : (j + 1) * slot, :] = jnp.where(chosen, 1.0, 0.0).astype(BF16)
        scales.append(jnp.sum(jnp.where(chosen, weights[j], 0.0), axis=1, keepdims=True))
    return jnp.concatenate(scales, axis=0)


def pick_kernel(sizes, width, grads, ins, ids_ref, *refs):
    send, slot = sizes
    refs, outs, sel_ref = refs[: -XN - 1], refs[-XN - 1 : -1], refs[-1]
    meta = jnp.concatenate(
        [refs[i][0:32, at + width : at + width + TOK].astype(F32) for i, at in grads], axis=1
    )
    scale = select_rows(ids_ref, meta, slot, sel_ref)
    over = width + TOK
    shared = all(i == k and at + over == to for (i, at), (k, to) in zip(grads, ins))

    def move(blocks, take, put, factor):
        rows = sum(
            jnp.dot(
                sel_ref[:, n * TOK : (n + 1) * TOK],
                refs[i][:, pl.ds(pl.multiple_of(at + take, TOK), TILE)],
                preferred_element_type=F32,
            )
            for n, (i, at) in enumerate(blocks)
        )
        if factor is not None:
            rows = rows * factor
        rows = rows.astype(BF16)
        for j in range(XN):
            outs[j][:, pl.ds(pl.multiple_of(put, TOK), TILE)] = rows[j * slot : j * slot + send]

    if shared:

        def both(low):
            second = (low >= width).astype(jnp.int32)
            factor = jnp.where(low >= width, jnp.ones_like(scale), scale)
            move(grads, low + second * TOK, low, factor)

        each_tile(2 * width // TILE, TILE, both)
    else:
        each_tile(width // TILE, TILE, lambda low: move(grads, low, low, scale))
        each_tile(width // TILE, TILE, lambda low: move(ins, low, width + low, None))


def pick(sizes, width, ids, grads, ins):
    arrays, places = [], []
    for blocks in (grads, ins):
        found = []
        for array, at in blocks:
            index = next((i for i, a in enumerate(arrays) if a is array), None)
            if index is None:
                index = len(arrays)
                arrays.append(array)
            found.append((index, at))
        places.append(tuple(found))
    send, slot = sizes
    total = len(grads) * TOK
    *rows, sel = run(
        functools.partial(pick_kernel, sizes, width, *places),
        [shaped(send, 2 * width)] * XN + [shaped(XN * slot, total)],
        [ids, *arrays],
        4 * XN * slot * total * width,
        XN * slot * width * 8,
        smem=1,
    )
    return rows, sel


def stack_rows(dst, parts, sizes, base):
    send, slot = sizes

    def step(low):
        for j, part in enumerate(parts):
            dst[(j + 1) * slot - 16 : (j + 1) * slot, pl.ds(low, TILE)] = jnp.zeros(
                (16, TILE), dst.dtype
            )
            dst[j * slot : j * slot + send, pl.ds(low, TILE)] = part[
                :, pl.ds(pl.multiple_of(base + low, TOK), TILE)
            ]

    each_tile(dst.shape[1] // TILE, TILE, step)


def expert_kernel(sizes, *refs):
    send, slot = sizes
    rows, (w_in, w_out) = refs[:XN], refs[XN : XN + 2]
    backs, (x_ref, g_ref, hidden_ref, pre_ref) = refs[XN + 2 : 2 * XN + 2], refs[2 * XN + 2 :]
    units, width = w_out.shape
    stack_rows(x_ref, rows, sizes, width)
    stack_rows(g_ref, rows, sizes, 0)

    def forward(low):
        high = pl.multiple_of(units + low, TOK)
        pair = jnp.concatenate([w_in[:, pl.ds(low, TOK)], w_in[:, pl.ds(high, TOK)]], axis=1)
        both = jnp.dot(x_ref[...], pair, preferred_element_type=F32)
        gate, upper = both[:, :TOK], both[:, TOK:]
        back = lax.dot_general(
            g_ref[...], w_out[pl.ds(low, TOK), :], NT, preferred_element_type=F32
        )
        sigma = 1.0 / (1.0 + jnp.exp(-gate))
        active = gate * sigma
        slope = sigma * (1.0 + gate * (1.0 - sigma))
        hidden_ref[:, pl.ds(low, TOK)] = (active * upper).astype(BF16)
        pre_ref[:, pl.ds(low, TOK)] = (back * upper * slope).astype(BF16)
        pre_ref[:, pl.ds(high, TOK)] = (back * active).astype(BF16)

    each_tile(units // TOK, TOK, forward)

    def backward(low):
        rows = lax.dot_general(
            pre_ref[...], w_in[pl.ds(low, HALF), :], NT, preferred_element_type=F32
        ).astype(BF16)
        for j in range(XN):
            backs[j][:, pl.ds(low, HALF)] = rows[j * slot : j * slot + send]

    each_tile(width // HALF, HALF, backward)


def expert(sizes, got, w_in, w_out):
    send, slot = sizes
    units, width = w_out.shape
    rows = XN * slot
    return run(
        functools.partial(expert_kernel, sizes),
        [shaped(send, width)] * XN
        + [shaped(rows, width)] * 2
        + [shaped(rows, units), shaped(rows, 2 * units)],
        [*got, w_in, w_out],
        10 * rows * units * width,
        rows * width * 8,
    )


def combine_kernel(sizes, adds, outs_at, sel_ref, *refs):
    send, slot = sizes
    backs, refs = refs[:XN], refs[XN:]
    incoming, refs = refs[: len(adds)], refs[len(adds) :]
    outs, stacked = refs[:-1], refs[-1]
    width = stacked.shape[1]

    def covers(ref, first, start, stop):
        return first <= start and stop <= first + ref.shape[1]

    def columns(first, low):
        return pl.ds(pl.multiple_of(low - first, TOK), TILE)

    whole = all(r.shape[1] == width for r in (*incoming, *outs))
    spans = [(0, width)] if whole else [(0, width // 2), (width // 2, width)]
    for start, stop in spans:

        def step(offset):
            low = pl.multiple_of(start + offset, TOK)
            here = pl.ds(low, TILE)
            for j, part in enumerate(backs):
                stacked[(j + 1) * slot - 16 : (j + 1) * slot, here] = jnp.zeros(
                    (16, TILE), stacked.dtype
                )
                stacked[j * slot : j * slot + send, here] = part[:, here]
            for out, (block, first) in zip(outs, outs_at):
                if not covers(out, first, start, stop):
                    continue
                total = lax.dot_general(
                    sel_ref[:, block * TOK : (block + 1) * TOK],
                    stacked[:, here],
                    TN,
                    preferred_element_type=F32,
                )
                for ref, (owner, begin) in zip(incoming, adds):
                    if owner == block and covers(ref, begin, start, stop):
                        total = total + ref[:, columns(begin, low)].astype(F32)
                out[:, columns(first, low)] = total.astype(out.dtype)

        each_tile((stop - start) // TILE, TILE, step)


def combine(sizes, sel, backs, incoming, adds, outs_at, outs):
    rows, total = sel.shape
    width = backs[0].shape[1]
    return run(
        functools.partial(combine_kernel, sizes, adds, outs_at),
        outs,
        [sel, *backs, *incoming],
        2 * rows * total * width,
        rows * width * 4,
        scratch=[pltpu.VMEM((rows, width), BF16)],
    )


def weight_kernel(count, turned, *refs):
    out = refs[-1]
    total = sum(
        lax.dot_general(a[...], b[...], TN, preferred_element_type=F32)
        for a, b in zip(refs[:count], refs[count : 2 * count])
    )
    out[...] = (total.T if turned else total).astype(BF16)


def weight_grads(wide, narrow, turned):
    tile = 256
    count = len(wide)
    width, units = wide[0].shape[1], narrow[0].shape[1]
    rows = sum(a.shape[0] for a in wide)
    return pl.pallas_call(
        functools.partial(weight_kernel, count, turned),
        grid=(width // tile,),
        in_specs=[pl.BlockSpec((a.shape[0], tile), lambda i: (0, i)) for a in wide]
        + [pl.BlockSpec(a.shape, lambda i: (0, 0)) for a in narrow],
        out_specs=pl.BlockSpec((units, tile), lambda i: (0, i))
        if turned
        else pl.BlockSpec((tile, units), lambda i: (i, 0)),
        out_shape=shaped(units, width) if turned else shaped(width, units),
        compiler_params=pltpu.CompilerParams(vmem_limit_bytes=VMEM_LIMIT),
        cost_estimate=pl.CostEstimate(
            flops=2 * rows * units * width, bytes_accessed=rows * width * 2, transcendentals=0
        ),
    )(*wide, *narrow)


def along_x(parts):
    moved = [parts[0]]
    for j in range(1, XN):
        pairs = [(x * ZN + z, (x ^ j) * ZN + z) for x in range(XN) for z in range(ZN)]
        moved.append(lax.ppermute(parts[j], "expert", pairs))
    return moved


def along_z(block, side):
    pairs = [
        (x * ZN + z, x * ZN + (((z + side) ^ 1) - side) % ZN)
        for x in range(XN)
        for z in range(ZN)
    ]
    return lax.ppermute(block, "expert", pairs)


def payload(grads, routes, probs):
    first = lax.reduce_precision(probs, 8, 7)
    rest = probs - first
    second = lax.reduce_precision(rest, 8, 7)
    third = rest - second
    table = jnp.concatenate([routes.astype(F32), first, second, third], axis=1).T
    meta = jnp.pad(table, ((0, TOK - table.shape[0]), (0, 0))).astype(BF16)
    return jnp.concatenate([grads, meta], axis=1)


def per_device(saved_inputs, grad_out, routes, route_probs, w_in, w_out):
    sections = lax.axis_size("pipe")
    width = saved_inputs.shape[2]
    half = width // 2
    over = width + TOK
    weight_in, weight_out = w_in[0, 0], w_out[0, 0]
    place = lax.axis_index("expert")
    column, depth = place // ZN, place % ZN
    ids = ((column ^ jnp.arange(XN, dtype=jnp.int32)) * ZN + depth)[None, :]
    sizes = [(round_up(CAP * n, 8), round_up(CAP * n, 16)) for n in (1, 2, 2, 2, 1)]

    own = lax.ppermute(saved_inputs[0], "pipe", [(i, sections - 1 - i) for i in range(sections)])
    pay = payload(grad_out[0], routes[0], route_probs[0])
    a1, b1 = along_z(pay, 0), along_z(pay, 1)
    a2, b2 = along_z(own, 0), along_z(own, 1)
    near_a, near_b = jnp.concatenate([a1, a2], axis=1), jnp.concatenate([b1, b2], axis=1)
    a3, b3 = along_z(near_b, 0), along_z(near_a, 1)
    a4, b4 = along_z(b3, 0), along_z(a3, 1)
    far_grads = along_z(b4[:, :over], 0)
    far_ins = along_z(a4[:, over:], 1)
    blocks = [([(pay, 0)], [(own, 0)])]
    blocks += [
        ([(a, 0), (b, 0)], [(a, over), (b, over)]) for a, b in ((near_a, near_b), (a3, b3), (a4, b4))
    ]
    blocks += [([(far_grads, 0)], [(far_ins, 0)])]
    sels, held, returned = [], [], []
    for n, (grads, ins) in enumerate(blocks):
        rows, sel = pick(sizes[n], width, ids, grads, ins)
        sels.append(sel)
        *backs, x_rows, g_rows, hidden, pre = expert(sizes[n], along_x(rows), weight_in, weight_out)
        held.append((x_rows, g_rows, hidden, pre))
        returned.append(along_x(backs))
    xs, gs, hs, ps = zip(*held)
    grad_w_in = weight_grads(xs, ps, False)
    grad_w_out = weight_grads(gs, hs, True)

    part, full = shaped(TOK, half), shaped(TOK, width)
    side_a, side_b = combine(
        sizes[4], sels[4], returned[4], [], (), ((0, 0), (0, half)), [part, part]
    )
    adds = ((1, 0), (0, half))
    for n in (3, 2, 1):
        incoming = [along_z(side_a, 0), along_z(side_b, 1)]
        side_a, side_b = combine(
            sizes[n], sels[n], returned[n], incoming, adds, ((0, 0), (1, 0)), [full, full]
        )
        adds = ((1, 0), (0, 0))
    incoming = [along_z(side_a, 0), along_z(side_b, 1)]
    (tokens,) = combine(
        sizes[0],
        sels[0],
        returned[0],
        incoming,
        ((0, 0), (0, 0)),
        ((0, 0),),
        [shaped(TOK, width, F32)],
    )
    return tokens[None], grad_w_in[None, None], grad_w_out[None, None]


def solution(mesh):
    rows = P("pipe", "expert", None)
    weights = P("pipe", "expert", None, None)
    return jax.shard_map(
        per_device,
        mesh=mesh,
        in_specs=(rows, rows, rows, rows, weights, weights),
        out_specs=(rows, weights, weights),
        check_vma=False,
    )
```

profile of v0, /device:TPU:16, one launch (start us, length us, event | category | flops | bytes accessed | tf_op | source)
XLA Modules:
  0.0 302.3 jit_solution(1128666304919147141)
XLA Ops:
  3.2 5.9 %collective-permute-start.9 = (bf16[128,2176]{1,0:T(8,128)(2,1)S(1)}, bf16[128,2176]{1,0:T(8,128)(2,1)S(1)}, u32[]{:S(2)}, u32[]{:S(2)}) collective-permute-start(bf16[128,2176]{1,0:T(8,128)(2,1)S(1)} %fusion.1.refs_0_), channel_id=1, source_target_pairs={{0,7},{1,2},{2,1},{3,4},{4,3},{5,6},{6,5},{7,0},{8,15},{9,10},{10,... | collective-permute-start | bytes 1671176 | tf_op jit(solution)/shard_map/ppermute | solution.py:304
  9.1 13.9 %collective-permute-done.refs_1_ = bf16[128,2048]{1,0:T(8,128)(2,1)S(1)} collective-permute-done((bf16[128,2048]{1,0:T(8,128)(2,1)S(1)}, bf16[128,2048]{1,0:T(8,128)(2,1)S(1)}, u32[]{:S(2)}, u32[]{:S(2)}) %collective-permute-start) | collective-permute-done | bytes 524320 | tf_op jit(solution)/shard_map/ppermute | solution.py:328
  24.3 13.7 %collective-permute-done.10 = bf16[128,2048]{1,0:T(8,128)(2,1)S(1)} collective-permute-done((bf16[128,2048]{1,0:T(8,128)(2,1)S(1)}, bf16[128,2048]{1,0:T(8,128)(2,1)S(1)}, u32[]{:S(2)}, u32[]{:S(2)}) %collective-permute-start.10) | collective-permute-done | bytes 524320 | tf_op jit(solution)/shard_map/ppermute | solution.py:304
  40.0 22.9 %collective-permute-done.17.refs_0_ = bf16[128,4224]{1,0:T(8,128)(2,1)} collective-permute-done((bf16[128,4224]{1,0:T(8,128)(2,1)S(1)}, bf16[128,4224]{1,0:T(8,128)(2,1)}, u32[]{:S(2)}, u32[]{:S(2)}) %collective-permute-start.17) | collective-permute-done | bytes 1081376 | tf_op jit(solution)/shard_map/ppermute | solution.py:304
  63.9 1.5 collective-permute-done.18.refs_1_
  65.4 1.7 collective-permute-start.25
  67.1 21.3 %collective-permute-done.26.refs_1_ = bf16[128,4224]{1,0:T(8,128)(2,1)S(1)} collective-permute-done((bf16[128,4224]{1,0:T(8,128)(2,1)}, bf16[128,4224]{1,0:T(8,128)(2,1)S(1)}, u32[]{:S(2)}, u32[]{:S(2)}) %collective-permute-start.26) | collective-permute-done | bytes 1081376 | tf_op jit(solution)/shard_map/ppermute | solution.py:304
  92.5 4.2 %shard_map.91 = (bf16[72,4096]{1,0:T(8,128)(2,1)S(1)}, bf16[72,4096]{1,0:T(8,128)(2,1)S(1)}, bf16[72,4096]{1,0:T(8,128)(2,1)S(1)}, bf16[72,4096]{1,0:T(8,128)(2,1)S(1)}, bf16[320,256]{1,0:T(8,128)(2,1)S(1)}) custom-call(s32[1,4]{1,0:T(1,128)S(1)} %multiply_add_fusion.ids_ref, bf16[128,4224]{1,0:T(8,128)(2,1)} %collective-permute-done.25.refs_0_, ...), custom_call_target="tpu_custom_call" | custom-call | flops 671088640 | bytes 5242880 | tf_op jit(solution)/shard_map/pallas_call | solution.py:33
  96.6 1.6 collective-permute-start.27
  98.2 5.7 %collective-permute-done.34.refs_1_ = bf16[128,2048]{1,0:T(8,128)(2,1)S(1)} collective-permute-done((bf16[128,2048]{1,0:T(8,128)(2,1)S(1)}, bf16[128,2048]{1,0:T(8,128)(2,1)S(1)}, u32[]{:S(2)}, u32[]{:S(2)}) %collective-permute-start.34) | collective-permute-done | bytes 524320 | tf_op jit(solution)/shard_map/ppermute | solution.py:304
  103.9 2.3 shard_map.93
  106.2 1.6 collective-permute-start.35
  107.8 2.7 collective-permute-start.28
  111.0 1.8 collective-permute-start.36
  112.8 2.3 collective-permute-start.37
  115.2 4.4 %shard_map.89 = (bf16[72,4096]{1,0:T(8,128)(2,1)S(1)}, bf16[72,4096]{1,0:T(8,128)(2,1)S(1)}, bf16[72,4096]{1,0:T(8,128)(2,1)S(1)}, bf16[72,4096]{1,0:T(8,128)(2,1)S(1)}, bf16[320,256]{1,0:T(8,128)(2,1)S(1)}) custom-call(s32[1,4]{1,0:T(1,128)S(1)} %multiply_add_fusion.ids_ref, bf16[128,4224]{1,0:T(8,128)(2,1)} %collective-permute-done.17.refs_0_, ...), custom_call_target="tpu_custom_call" | custom-call | flops 671088640 | bytes 5242880 | tf_op jit(solution)/shard_map/pallas_call | solution.py:33
  120.9 20.4 %collective-permute-done.36.refs_2_ = bf16[40,4096]{1,0:T(8,128)(2,1)S(1)} collective-permute-done((bf16[40,4096]{1,0:T(8,128)(2,1)S(1)}, bf16[40,4096]{1,0:T(8,128)(2,1)S(1)}, u32[]{:S(2)}, u32[]{:S(2)}) %collective-permute-start.36) | collective-permute-done | bytes 327712 | tf_op jit(solution)/shard_map/ppermute | solution.py:294
  142.1 19.2 %collective-permute-done.37.refs_3_ = bf16[40,4096]{1,0:T(8,128)(2,1)S(1)} collective-permute-done((bf16[40,4096]{1,0:T(8,128)(2,1)S(1)}, bf16[40,4096]{1,0:T(8,128)(2,1)S(1)}, u32[]{:S(2)}, u32[]{:S(2)}) %collective-permute-start.37) | collective-permute-done | bytes 327712 | tf_op jit(solution)/shard_map/ppermute | solution.py:294
  161.9 4.4 %shard_map.94 = (bf16[40,2048]{1,0:T(8,128)(2,1)S(1)}, bf16[40,2048]{1,0:T(8,128)(2,1)S(1)}, bf16[40,2048]{1,0:T(8,128)(2,1)S(1)}, bf16[40,2048]{1,0:T(8,128)(2,...) custom-call(bf16[40,4096]{1,0:T(8,128)(2,1)S(1)} %get-tuple-element., ...), custom_call_target="tpu_custom_call" | custom-call | flops 1509949440 | bytes 3145728 | tf_op jit(solution)/shard_map/pallas_call | solution.py:33
  166.4 5.5 %shard_map.92 = (bf16[72,2048]{1,0:T(8,128)(2,1)S(1)}, bf16[72,2048]{1,0:T(8,128)(2,1)S(1)}, bf16[72,2048]{1,0:T(8,128)(2,1)S(1)}, bf16[72,2048]{1,0:T(8,128)(2,...) custom-call(bf16[72,4096]{1,0:T(8,128)(2,1)S(1)} %get-tuple-element., ...), custom_call_target="tpu_custom_call" | custom-call | flops 2516582400 | bytes 5242880 | tf_op jit(solution)/shard_map/pallas_call | solution.py:33
  171.9 2.1 collective-permute-start.30
  174.0 2.3 collective-permute-start.39
  176.9 3.4 %shard_map.87 = (bf16[72,4096]{1,0:T(8,128)(2,1)S(1)}, bf16[72,4096]{1,0:T(8,128)(2,1)S(1)}, bf16[72,4096]{1,0:T(8,128)(2,1)S(1)}, bf16[72,4096]{1,0:T(8,128)(2,1)S(1)}, bf16[320,256]{1,0:T(8,128)(2,1)S(1)}) custom-call(s32[1,4]{1,0:T(1,128)S(1)} %multiply_add_fusion.ids_ref, bf16[128,4224]{1,0:T(8,128)(2,1)S(1)} %constant_dynamic-update-slice_fusion.refs_0_, ...), custom_call_target="tpu_custom_call" | custom-call | flops 671088640 | bytes 5242880 | tf_op jit(solution)/shard_map/pallas_call | solution.py:33
  180.2 7.5 %collective-permute-done.39.refs_2_ = bf16[40,2048]{1,0:T(8,128)(2,1)S(1)} collective-permute-done((bf16[40,2048]{1,0:T(8,128)(2,1)S(1)}, bf16[40,2048]{1,0:T(8,128)(2,1)S(1)}, u32[]{:S(2)}, u32[]{:S(2)}) %collective-permute-start.39) | collective-permute-done | bytes 163872 | tf_op jit(solution)/shard_map/ppermute | solution.py:294
  187.8 1.7 collective-permute-done.40.refs_3_
  190.5 2.9 collective-permute-start.32
  193.5 5.5 %shard_map.90 = (bf16[72,2048]{1,0:T(8,128)(2,1)S(1)}, bf16[72,2048]{1,0:T(8,128)(2,1)S(1)}, bf16[72,2048]{1,0:T(8,128)(2,1)S(1)}, bf16[72,2048]{1,0:T(8,128)(2,...) custom-call(bf16[72,4096]{1,0:T(8,128)(2,1)S(1)} %get-tuple-element., ...), custom_call_target="tpu_custom_call" | custom-call | flops 2516582400 | bytes 5242880 | tf_op jit(solution)/shard_map/pallas_call | solution.py:33
  199.0 10.8 %collective-permute-done.31.refs_2_ = bf16[72,2048]{1,0:T(8,128)(2,1)S(1)} collective-permute-done((bf16[72,2048]{1,0:T(8,128)(2,1)S(1)}, bf16[72,2048]{1,0:T(8,128)(2,1)S(1)}, u32[]{:S(2)}, u32[]{:S(2)}) %collective-permute-start.31) | collective-permute-done | bytes 294944 | tf_op jit(solution)/shard_map/ppermute | solution.py:294
  210.3 4.2 %collective-permute-start.23 = (bf16[72,2048]{1,0:T(8,128)(2,1)S(1)}, bf16[72,2048]{1,0:T(8,128)(2,1)S(1)}, u32[]{:S(2)}, u32[]{:S(2)}) collective-permute-start(bf16[72,2048]{1,0:T(8,128)(2,1)S(1)} %get-tuple-element.101), channel_id=1, source_target_pairs={{0,16},{1,17},{2,18},{3,19},{4,20},{5,21},{6,22},{7,23},{8,24},{9,... | collective-permute-start | bytes 884744 | tf_op jit(solution)/shard_map/ppermute | solution.py:294
  216.5 3.2 %collective-permute-start.13 = (bf16[72,4096]{1,0:T(8,128)(2,1)S(1)}, bf16[72,4096]{1,0:T(8,128)(2,1)S(1)}, u32[]{:S(2)}, u32[]{:S(2)}) collective-permute-start(bf16[72,4096]{1,0:T(8,128)(2,1)S(1)} %get-tuple-element.89), channel_id=1, source_target_pairs={{0,24},{1,25},{2,26},{3,27},{4,28},{5,29},{6,30},{7,31},{8,16},{9,... | collective-permute-start | bytes 1769480 | tf_op jit(solution)/shard_map/ppermute | solution.py:294
  219.7 2.7 collective-permute-done.23.refs_2_
  222.5 2.3 shard_map.85
  224.8 16.4 %collective-permute-done.24.refs_3_ = bf16[72,2048]{1,0:T(8,128)(2,1)S(1)} collective-permute-done((bf16[72,2048]{1,0:T(8,128)(2,1)S(1)}, bf16[72,2048]{1,0:T(8,128)(2,1)S(1)}, u32[]{:S(2)}, u32[]{:S(2)}) %collective-permute-start.24) | collective-permute-done | bytes 294944 | tf_op jit(solution)/shard_map/ppermute | solution.py:294
  241.1 1.4 collective-permute-start.1
  243.9 1.9 collective-permute-start.3
  247.2 4.5 %collective-permute-start.45 = (bf16[128,2048]{1,0:T(8,128)(2,1)S(1)}, bf16[128,2048]{1,0:T(8,128)(2,1)S(1)}, u32[]{:S(2)}, u32[]{:S(2)}) collective-permute-start(bf16[128,2048]{1,0:T(8,128)(2,1)S(1)} %get-tuple-element.125), channel_id=1, source_target_pairs={{0,1},{1,0},{2,3},{3,2},{4,5},{5,4},{6,7},{7,6},{8,9},{9,8},{10,11... | collective-permute-start | bytes 1572872 | tf_op jit(solution)/shard_map/ppermute | solution.py:304
  251.7 1.5 collective-permute-start.46
  253.2 5.6 %shard_map.88 = (bf16[72,2048]{1,0:T(8,128)(2,1)S(1)}, bf16[72,2048]{1,0:T(8,128)(2,1)S(1)}, bf16[72,2048]{1,0:T(8,128)(2,1)S(1)}, bf16[72,2048]{1,0:T(8,128)(2,...) custom-call(bf16[72,4096]{1,0:T(8,128)(2,1)S(1)} %get-tuple-element., ...), custom_call_target="tpu_custom_call" | custom-call | flops 2516582400 | bytes 5242880 | tf_op jit(solution)/shard_map/pallas_call | solution.py:33
  258.9 1.9 collective-permute-start.15
  260.8 2.8 collective-permute-start.16
  263.6 4.4 %shard_map.86 = (bf16[40,2048]{1,0:T(8,128)(2,1)S(1)}, bf16[40,2048]{1,0:T(8,128)(2,1)S(1)}, bf16[40,2048]{1,0:T(8,128)(2,1)S(1)}, bf16[40,2048]{1,0:T(8,128)(2,...) custom-call(bf16[40,4096]{1,0:T(8,128)(2,1)S(1)} %get-tuple-element., ...), custom_call_target="tpu_custom_call" | custom-call | flops 1509949440 | bytes 3145728 | tf_op jit(solution)/shard_map/pallas_call | solution.py:33
  268.1 3.6 %collective-permute-done.15.refs_2_ = bf16[72,2048]{1,0:T(8,128)(2,1)S(1)} collective-permute-done((bf16[72,2048]{1,0:T(8,128)(2,1)S(1)}, bf16[72,2048]{1,0:T(8,128)(2,1)S(1)}, u32[]{:S(2)}, u32[]{:S(2)}) %collective-permute-start.15) | collective-permute-done | bytes 294944 | tf_op jit(solution)/shard_map/ppermute | solution.py:294
  272.1 2.8 collective-permute-done.16.refs_3_
  277.2 4.2 %collective-permute-start.47 = (bf16[128,2048]{1,0:T(8,128)(2,1)S(1)}, bf16[128,2048]{1,0:T(8,128)(2,1)S(1)}, u32[]{:S(2)}, u32[]{:S(2)}) collective-permute-start(bf16[128,2048]{1,0:T(8,128)(2,1)S(1)} %get-tuple-element.127), channel_id=1, source_target_pairs={{0,1},{1,0},{2,3},{3,2},{4,5},{5,4},{6,7},{7,6},{8,9},{9,8},{10,11... | collective-permute-start | bytes 1572872 | tf_op jit(solution)/shard_map/ppermute | solution.py:304
  281.4 1.5 collective-permute-start.48
  282.9 9.7 %shard_map.100 = bf16[2048,768]{1,0:T(8,128)(2,1)} custom-call(bf16[192,2048]{1,0:T(8,128)(2,1)S(1)} %get-tuple-element.129.refs_0_, bf16[320,2048]{1,0:T(8,128)(2,1)S(1)} %get-tuple-element.130.refs_1_, bf16[320,2048]{1,0:T(8,128)(2,1)S(1)} %get-tuple-element.131.refs_2_, bf16[320,2048]{1,0:T(8,128)(2,1)S(1)} %get-tuple-element.132.refs_3_, ...), custom_call_target="tpu_custom_call" | custom-call | flops 4227858432 | bytes 5505024 | tf_op jit(solution)/shard_map/pallas_call | solution.py:274
  292.6 7.8 %shard_map.101 = bf16[384,2048]{1,0:T(8,128)(2,1)} custom-call(bf16[192,2048]{1,0:T(8,128)(2,1)S(1)} %get-tuple-element.139.refs_0_, bf16[320,2048]{1,0:T(8,128)(2,1)S(1)} %get-tuple-element.140.refs_1_, bf16[320,2048]{1,0:T(8,128)(2,1)S(1)} %get-tuple-element.141.refs_2_, bf16[320,2048]{1,0:T(8,128)(2,1)S(1)} %get-tuple-element.142.refs_3_, ...), custom_call_target="tpu_custom_call" | custom-call | flops 2113929216 | bytes 5505024 | tf_op jit(solution)/shard_map/pallas_call | solution.py:274
  300.4 1.8 shard_map.99
  (88 shorter events, 23.8 us)
Async XLA Ops:
  3.2 20.3 %collective-permute-start.9 = (bf16[128,2176]{1,0:T(8,128)(2,1)S(1)}, bf16[128,2176]{1,0:T(8,128)(2,1)S(1)}, u32[]{:S(2)}, u32[]{:S(2)}) collective-permute-start(bf16[128,2176]{1,0:T(8,128)(2,1)S(1)} %fusion.1.refs_0_), channel_id=1, source_target_pairs={{0,7},{1,2},{2,1},{3,4},{4,3},{5,6},{6,5},{7,0},{8,15},{9,10},{10,... | collective-permute-start | bytes 1671176 | tf_op jit(solution)/shard_map/ppermute | solution.py:304
  9.1 14.0 %collective-permute-start = (bf16[128,2048]{1,0:T(8,128)(2,1)S(1)}, bf16[128,2048]{1,0:T(8,128)(2,1)S(1)}, u32[]{:S(2)}, u32[]{:S(2)}) collective-permute-start(bf16[128,2048]{1,0:T(8,128)(2,1)S(1)} %bitcast.31), channel_id=1, source_target_pairs={{0,224},{32,192},{64,160},{96,128},{128,96},{160,64},{192,32},{224... | collective-permute-start | bytes 1572872 | tf_op jit(solution)/shard_map/ppermute | solution.py:328
  9.1 15.1 %collective-permute-start.7 = (bf16[128,2176]{1,0:T(8,128)(2,1)S(1)}, bf16[128,2176]{1,0:T(8,128)(2,1)S(1)}, u32[]{:S(2)}, u32[]{:S(2)}) collective-permute-start(bf16[128,2176]{1,0:T(8,128)(2,1)S(1)} %fusion.1.refs_0_), channel_id=1, source_target_pairs={{0,1},{1,0},{2,3},{3,2},{4,5},{5,4},{6,7},{7,6},{8,9},{9,8},{10,11... | collective-permute-start | bytes 1671176 | tf_op jit(solution)/shard_map/ppermute | solution.py:304
  23.1 14.9 %collective-permute-start.10 = (bf16[128,2048]{1,0:T(8,128)(2,1)S(1)}, bf16[128,2048]{1,0:T(8,128)(2,1)S(1)}, u32[]{:S(2)}, u32[]{:S(2)}) collective-permute-start(bf16[128,2048]{1,0:T(8,128)(2,1)S(1)} %collective-permute-done.refs_1_), channel_id=1, source_target_pairs={{0,7},{1,2},{2,1},{3,4},{4,3},{5,6},{6,5},{7,0},{8,15},{9,10},{10,... | collective-permute-start | bytes 1572872 | tf_op jit(solution)/shard_map/ppermute | solution.py:304
  23.4 15.7 %collective-permute-start.8 = (bf16[128,2048]{1,0:T(8,128)(2,1)S(1)}, bf16[128,2048]{1,0:T(8,128)(2,1)S(1)}, u32[]{:S(2)}, u32[]{:S(2)}) collective-permute-start(bf16[128,2048]{1,0:T(8,128)(2,1)S(1)} %collective-permute-done.refs_1_), channel_id=1, source_target_pairs={{0,1},{1,0},{2,3},{3,2},{4,5},{5,4},{6,7},{7,6},{8,9},{9,8},{10,11... | collective-permute-start | bytes 1572872 | tf_op jit(solution)/shard_map/ppermute | solution.py:304
  38.0 24.9 %collective-permute-start.17 = (bf16[128,4224]{1,0:T(8,128)(2,1)S(1)}, bf16[128,4224]{1,0:T(8,128)(2,1)}, u32[]{:S(2)}, u32[]{:S(2)}) collective-permute-start(bf16[128,4224]{1,0:T(8,128)(2,1)S(1)} %constant_dynamic-update-slice_fusion.2.refs_1_), channel_id=1, source_target_pairs={{0,1},{1,0},{2,3},{3,2},{4,5},{5,4},{6,7},{7,6},{8,9},{9,8},{10,11... | collective-permute-start | bytes 3244040 | tf_op jit(solution)/shard_map/ppermute | solution.py:304
  39.1 26.2 %collective-permute-start.18 = (bf16[128,4224]{1,0:T(8,128)(2,1)S(1)}, bf16[128,4224]{1,0:T(8,128)(2,1)}, u32[]{:S(2)}, u32[]{:S(2)}) collective-permute-start(bf16[128,4224]{1,0:T(8,128)(2,1)S(1)} %constant_dynamic-update-slice_fusion.refs_0_), channel_id=1, source_target_pairs={{0,7},{1,2},{2,1},{3,4},{4,3},{5,6},{6,5},{7,0},{8,15},{9,10},{10,... | collective-permute-start | bytes 3244040 | tf_op jit(solution)/shard_map/ppermute | solution.py:304
  63.0 25.4 %collective-permute-start.26 = (bf16[128,4224]{1,0:T(8,128)(2,1)}, bf16[128,4224]{1,0:T(8,128)(2,1)S(1)}, u32[]{:S(2)}, u32[]{:S(2)}) collective-permute-start(bf16[128,4224]{1,0:T(8,128)(2,1)} %collective-permute-done.17.refs_0_), channel_id=1, source_target_pairs={{0,7},{1,2},{2,1},{3,4},{4,3},{5,6},{6,5},{7,0},{8,15},{9,10},{10,... | collective-permute-start | bytes 3244040 | tf_op jit(solution)/shard_map/ppermute | solution.py:304
  65.4 24.8 %collective-permute-start.25 = (bf16[128,4224]{1,0:T(8,128)(2,1)}, bf16[128,4224]{1,0:T(8,128)(2,1)}, u32[]{:S(2)}, u32[]{:S(2)}) collective-permute-start(bf16[128,4224]{1,0:T(8,128)(2,1)} %collective-permute-done.18.refs_1_), channel_id=1, source_target_pairs={{0,1},{1,0},{2,3},{3,2},{4,5},{5,4},{6,7},{7,6},{8,9},{9,8},{10,11... | collective-permute-start | bytes 3244040 | tf_op jit(solution)/shard_map/ppermute | solution.py:304
  88.4 15.5 %collective-permute-start.33 = (bf16[128,2176]{1,0:T(8,128)(2,1)S(1)}, bf16[128,2176]{1,0:T(8,128)(2,1)S(1)}, u32[]{:S(2)}, u32[]{:S(2)}) collective-permute-start(bf16[128,2176]{1,0:T(8,128)(2,1)S(1)} %slice.8), channel_id=1, source_target_pairs={{0,1},{1,0},{2,3},{3,2},{4,5},{5,4},{6,7},{7,6},{8,9},{9,8},{10,11... | collective-permute-start | bytes 1671176 | tf_op jit(solution)/shard_map/ppermute | solution.py:304
  91.2 12.6 %collective-permute-start.34 = (bf16[128,2048]{1,0:T(8,128)(2,1)S(1)}, bf16[128,2048]{1,0:T(8,128)(2,1)S(1)}, u32[]{:S(2)}, u32[]{:S(2)}) collective-permute-start(bf16[128,2048]{1,0:T(8,128)(2,1)S(1)} %slice.9), channel_id=1, source_target_pairs={{0,7},{1,2},{2,1},{3,4},{4,3},{5,6},{6,5},{7,0},{8,15},{9,10},{10,... | collective-permute-start | bytes 1572872 | tf_op jit(solution)/shard_map/ppermute | solution.py:304
  96.6 16.2 %collective-permute-start.27 = (bf16[72,4096]{1,0:T(8,128)(2,1)S(1)}, bf16[72,4096]{1,0:T(8,128)(2,1)S(1)}, u32[]{:S(2)}, u32[]{:S(2)}) collective-permute-start(bf16[72,4096]{1,0:T(8,128)(2,1)S(1)} %get-tuple-element.105), channel_id=1, source_target_pairs={{0,8},{1,9},{2,10},{3,11},{4,12},{5,13},{6,14},{7,15},{8,0},{9,1},... | collective-permute-start | bytes 1769480 | tf_op jit(solution)/shard_map/ppermute | solution.py:294
  106.2 13.3 %collective-permute-start.35 = (bf16[40,4096]{1,0:T(8,128)(2,1)S(1)}, bf16[40,4096]{1,0:T(8,128)(2,1)S(1)}, u32[]{:S(2)}, u32[]{:S(2)}) collective-permute-start(bf16[40,4096]{1,0:T(8,128)(2,1)S(1)} %get-tuple-element.114), channel_id=1, source_target_pairs={{0,8},{1,9},{2,10},{3,11},{4,12},{5,13},{6,14},{7,15},{8,0},{9,1},... | collective-permute-start | bytes 983048 | tf_op jit(solution)/shard_map/ppermute | solution.py:294
  107.8 58.5 %collective-permute-start.28 = (bf16[72,4096]{1,0:T(8,128)(2,1)S(1)}, bf16[72,4096]{1,0:T(8,128)(2,1)S(1)}, u32[]{:S(2)}, u32[]{:S(2)}) collective-permute-start(bf16[72,4096]{1,0:T(8,128)(2,1)S(1)} %get-tuple-element.106), channel_id=1, source_target_pairs={{0,16},{1,17},{2,18},{3,19},{4,20},{5,21},{6,22},{7,23},{8,24},{9,... | collective-permute-start | bytes 1769480 | tf_op jit(solution)/shard_map/ppermute | solution.py:294
  110.5 55.9 %collective-permute-start.29 = (bf16[72,4096]{1,0:T(8,128)(2,1)S(1)}, bf16[72,4096]{1,0:T(8,128)(2,1)S(1)}, u32[]{:S(2)}, u32[]{:S(2)}) collective-permute-start(bf16[72,4096]{1,0:T(8,128)(2,1)S(1)} %get-tuple-element.107), channel_id=1, source_target_pairs={{0,24},{1,25},{2,26},{3,27},{4,28},{5,29},{6,30},{7,31},{8,16},{9,... | collective-permute-start | bytes 1769480 | tf_op jit(solution)/shard_map/ppermute | solution.py:294
  111.0 30.3 %collective-permute-start.36 = (bf16[40,4096]{1,0:T(8,128)(2,1)S(1)}, bf16[40,4096]{1,0:T(8,128)(2,1)S(1)}, u32[]{:S(2)}, u32[]{:S(2)}) collective-permute-start(bf16[40,4096]{1,0:T(8,128)(2,1)S(1)} %get-tuple-element.115), channel_id=1, source_target_pairs={{0,16},{1,17},{2,18},{3,19},{4,20},{5,21},{6,22},{7,23},{8,24},{9,... | collective-permute-start | bytes 983048 | tf_op jit(solution)/shard_map/ppermute | solution.py:294
  112.8 48.5 %collective-permute-start.37 = (bf16[40,4096]{1,0:T(8,128)(2,1)S(1)}, bf16[40,4096]{1,0:T(8,128)(2,1)S(1)}, u32[]{:S(2)}, u32[]{:S(2)}) collective-permute-start(bf16[40,4096]{1,0:T(8,128)(2,1)S(1)} %get-tuple-element.116), channel_id=1, source_target_pairs={{0,24},{1,25},{2,26},{3,27},{4,28},{5,29},{6,30},{7,31},{8,16},{9,... | collective-permute-start | bytes 983048 | tf_op jit(solution)/shard_map/ppermute | solution.py:294
  119.6 54.5 %collective-permute-start.19 = (bf16[72,4096]{1,0:T(8,128)(2,1)S(1)}, bf16[72,4096]{1,0:T(8,128)(2,1)S(1)}, u32[]{:S(2)}, u32[]{:S(2)}) collective-permute-start(bf16[72,4096]{1,0:T(8,128)(2,1)S(1)} %get-tuple-element.96), channel_id=1, source_target_pairs={{0,8},{1,9},{2,10},{3,11},{4,12},{5,13},{6,14},{7,15},{8,0},{9,1},... | collective-permute-start | bytes 1769480 | tf_op jit(solution)/shard_map/ppermute | solution.py:294
  141.3 49.2 %collective-permute-start.20 = (bf16[72,4096]{1,0:T(8,128)(2,1)S(1)}, bf16[72,4096]{1,0:T(8,128)(2,1)S(1)}, u32[]{:S(2)}, u32[]{:S(2)}) collective-permute-start(bf16[72,4096]{1,0:T(8,128)(2,1)S(1)} %get-tuple-element.97), channel_id=1, source_target_pairs={{0,16},{1,17},{2,18},{3,19},{4,20},{5,21},{6,22},{7,23},{8,24},{9,... | collective-permute-start | bytes 1769480 | tf_op jit(solution)/shard_map/ppermute | solution.py:294
  161.4 32.0 %collective-permute-start.21 = (bf16[72,4096]{1,0:T(8,128)(2,1)S(1)}, bf16[72,4096]{1,0:T(8,128)(2,1)S(1)}, u32[]{:S(2)}, u32[]{:S(2)}) collective-permute-start(bf16[72,4096]{1,0:T(8,128)(2,1)S(1)} %get-tuple-element.98), channel_id=1, source_target_pairs={{0,24},{1,25},{2,26},{3,27},{4,28},{5,29},{6,30},{7,31},{8,16},{9,... | collective-permute-start | bytes 1769480 | tf_op jit(solution)/shard_map/ppermute | solution.py:294
  166.3 10.0 %collective-permute-start.38 = (bf16[40,2048]{1,0:T(8,128)(2,1)S(1)}, bf16[40,2048]{1,0:T(8,128)(2,1)S(1)}, u32[]{:S(2)}, u32[]{:S(2)}) collective-permute-start(bf16[40,2048]{1,0:T(8,128)(2,1)S(1)} %get-tuple-element.118), channel_id=1, source_target_pairs={{0,8},{1,9},{2,10},{3,11},{4,12},{5,13},{6,14},{7,15},{8,0},{9,1},... | collective-permute-start | bytes 491528 | tf_op jit(solution)/shard_map/ppermute | solution.py:294
  171.9 21.4 %collective-permute-start.30 = (bf16[72,2048]{1,0:T(8,128)(2,1)S(1)}, bf16[72,2048]{1,0:T(8,128)(2,1)S(1)}, u32[]{:S(2)}, u32[]{:S(2)}) collective-permute-start(bf16[72,2048]{1,0:T(8,128)(2,1)S(1)} %get-tuple-element.109), channel_id=1, source_target_pairs={{0,8},{1,9},{2,10},{3,11},{4,12},{5,13},{6,14},{7,15},{8,0},{9,1},... | collective-permute-start | bytes 884744 | tf_op jit(solution)/shard_map/ppermute | solution.py:294
  174.0 13.7 %collective-permute-start.39 = (bf16[40,2048]{1,0:T(8,128)(2,1)S(1)}, bf16[40,2048]{1,0:T(8,128)(2,1)S(1)}, u32[]{:S(2)}, u32[]{:S(2)}) collective-permute-start(bf16[40,2048]{1,0:T(8,128)(2,1)S(1)} %get-tuple-element.119), channel_id=1, source_target_pairs={{0,16},{1,17},{2,18},{3,19},{4,20},{5,21},{6,22},{7,23},{8,24},{9,... | collective-permute-start | bytes 491528 | tf_op jit(solution)/shard_map/ppermute | solution.py:294
  176.3 13.2 %collective-permute-start.40 = (bf16[40,2048]{1,0:T(8,128)(2,1)S(1)}, bf16[40,2048]{1,0:T(8,128)(2,1)S(1)}, u32[]{:S(2)}, u32[]{:S(2)}) collective-permute-start(bf16[40,2048]{1,0:T(8,128)(2,1)S(1)} %get-tuple-element.120), channel_id=1, source_target_pairs={{0,24},{1,25},{2,26},{3,27},{4,28},{5,29},{6,30},{7,31},{8,16},{9,... | collective-permute-start | bytes 491528 | tf_op jit(solution)/shard_map/ppermute | solution.py:294
  187.7 28.3 %collective-permute-start.11 = (bf16[72,4096]{1,0:T(8,128)(2,1)S(1)}, bf16[72,4096]{1,0:T(8,128)(2,1)S(1)}, u32[]{:S(2)}, u32[]{:S(2)}) collective-permute-start(bf16[72,4096]{1,0:T(8,128)(2,1)S(1)} %get-tuple-element.87), channel_id=1, source_target_pairs={{0,8},{1,9},{2,10},{3,11},{4,12},{5,13},{6,14},{7,15},{8,0},{9,1},... | collective-permute-start | bytes 1769480 | tf_op jit(solution)/shard_map/ppermute | solution.py:294
  189.5 20.3 %collective-permute-start.31 = (bf16[72,2048]{1,0:T(8,128)(2,1)S(1)}, bf16[72,2048]{1,0:T(8,128)(2,1)S(1)}, u32[]{:S(2)}, u32[]{:S(2)}) collective-permute-start(bf16[72,2048]{1,0:T(8,128)(2,1)S(1)} %get-tuple-element.110), channel_id=1, source_target_pairs={{0,16},{1,17},{2,18},{3,19},{4,20},{5,21},{6,22},{7,23},{8,24},{9,... | collective-permute-start | bytes 884744 | tf_op jit(solution)/shard_map/ppermute | solution.py:294
  190.5 19.8 %collective-permute-start.32 = (bf16[72,2048]{1,0:T(8,128)(2,1)S(1)}, bf16[72,2048]{1,0:T(8,128)(2,1)S(1)}, u32[]{:S(2)}, u32[]{:S(2)}) collective-permute-start(bf16[72,2048]{1,0:T(8,128)(2,1)S(1)} %get-tuple-element.111), channel_id=1, source_target_pairs={{0,24},{1,25},{2,26},{3,27},{4,28},{5,29},{6,30},{7,31},{8,16},{9,... | collective-permute-start | bytes 884744 | tf_op jit(solution)/shard_map/ppermute | solution.py:294
  193.4 21.1 %collective-permute-start.41 = (bf16[128,1024]{1,0:T(8,128)(2,1)S(1)}, bf16[128,1024]{1,0:T(8,128)(2,1)S(1)}, u32[]{:S(2)}, u32[]{:S(2)}) collective-permute-start(bf16[128,1024]{1,0:T(8,128)(2,1)S(1)} %get-tuple-element.121), channel_id=1, source_target_pairs={{0,1},{1,0},{2,3},{3,2},{4,5},{5,4},{6,7},{7,6},{8,9},{9,8},{10,11... | collective-permute-start | bytes 786440 | tf_op jit(solution)/shard_map/ppermute | solution.py:304
  193.4 21.1 %collective-permute-start.42 = (bf16[128,1024]{1,0:T(8,128)(2,1)S(1)}, bf16[128,1024]{1,0:T(8,128)(2,1)S(1)}, u32[]{:S(2)}, u32[]{:S(2)}) collective-permute-start(bf16[128,1024]{1,0:T(8,128)(2,1)S(1)} %get-tuple-element.122), channel_id=1, source_target_pairs={{0,7},{1,2},{2,1},{3,4},{4,3},{5,6},{6,5},{7,0},{8,15},{9,10},{10,... | collective-permute-start | bytes 786440 | tf_op jit(solution)/shard_map/ppermute | solution.py:304
  210.3 12.1 %collective-permute-start.23 = (bf16[72,2048]{1,0:T(8,128)(2,1)S(1)}, bf16[72,2048]{1,0:T(8,128)(2,1)S(1)}, u32[]{:S(2)}, u32[]{:S(2)}) collective-permute-start(bf16[72,2048]{1,0:T(8,128)(2,1)S(1)} %get-tuple-element.101), channel_id=1, source_target_pairs={{0,16},{1,17},{2,18},{3,19},{4,20},{5,21},{6,22},{7,23},{8,24},{9,... | collective-permute-start | bytes 884744 | tf_op jit(solution)/shard_map/ppermute | solution.py:294
  215.8 26.7 %collective-permute-start.43 = (bf16[128,2048]{1,0:T(8,128)(2,1)S(1)}, bf16[128,2048]{1,0:T(8,128)(2,1)S(1)}, u32[]{:S(2)}, u32[]{:S(2)}) collective-permute-start(bf16[128,2048]{1,0:T(8,128)(2,1)S(1)} %get-tuple-element.123), channel_id=1, source_target_pairs={{0,1},{1,0},{2,3},{3,2},{4,5},{5,4},{6,7},{7,6},{8,9},{9,8},{10,11... | collective-permute-start | bytes 1572872 | tf_op jit(solution)/shard_map/ppermute | solution.py:304
  215.9 28.0 %collective-permute-start.44 = (bf16[128,2048]{1,0:T(8,128)(2,1)S(1)}, bf16[128,2048]{1,0:T(8,128)(2,1)S(1)}, u32[]{:S(2)}, u32[]{:S(2)}) collective-permute-start(bf16[128,2048]{1,0:T(8,128)(2,1)S(1)} %get-tuple-element.124), channel_id=1, source_target_pairs={{0,7},{1,2},{2,1},{3,4},{4,3},{5,6},{6,5},{7,0},{8,15},{9,10},{10,... | collective-permute-start | bytes 1572872 | tf_op jit(solution)/shard_map/ppermute | solution.py:304
  216.1 31.1 %collective-permute-start.12 = (bf16[72,4096]{1,0:T(8,128)(2,1)S(1)}, bf16[72,4096]{1,0:T(8,128)(2,1)S(1)}, u32[]{:S(2)}, u32[]{:S(2)}) collective-permute-start(bf16[72,4096]{1,0:T(8,128)(2,1)S(1)} %get-tuple-element.88), channel_id=1, source_target_pairs={{0,16},{1,17},{2,18},{3,19},{4,20},{5,21},{6,22},{7,23},{8,24},{9,... | collective-permute-start | bytes 1769480 | tf_op jit(solution)/shard_map/ppermute | solution.py:294
  216.5 35.2 %collective-permute-start.13 = (bf16[72,4096]{1,0:T(8,128)(2,1)S(1)}, bf16[72,4096]{1,0:T(8,128)(2,1)S(1)}, u32[]{:S(2)}, u32[]{:S(2)}) collective-permute-start(bf16[72,4096]{1,0:T(8,128)(2,1)S(1)} %get-tuple-element.89), channel_id=1, source_target_pairs={{0,24},{1,25},{2,26},{3,27},{4,28},{5,29},{6,30},{7,31},{8,16},{9,... | collective-permute-start | bytes 1769480 | tf_op jit(solution)/shard_map/ppermute | solution.py:294
  222.4 18.7 %collective-permute-start.24 = (bf16[72,2048]{1,0:T(8,128)(2,1)S(1)}, bf16[72,2048]{1,0:T(8,128)(2,1)S(1)}, u32[]{:S(2)}, u32[]{:S(2)}) collective-permute-start(bf16[72,2048]{1,0:T(8,128)(2,1)S(1)} %get-tuple-element.102), channel_id=1, source_target_pairs={{0,24},{1,25},{2,26},{3,27},{4,28},{5,29},{6,30},{7,31},{8,16},{9,... | collective-permute-start | bytes 884744 | tf_op jit(solution)/shard_map/ppermute | solution.py:294
  241.1 17.7 %collective-permute-start.1 = (bf16[40,4096]{1,0:T(8,128)(2,1)S(1)}, bf16[40,4096]{1,0:T(8,128)(2,1)S(1)}, u32[]{:S(2)}, u32[]{:S(2)}) collective-permute-start(bf16[40,4096]{1,0:T(8,128)(2,1)S(1)} %get-tuple-element.78), channel_id=1, source_target_pairs={{0,8},{1,9},{2,10},{3,11},{4,12},{5,13},{6,14},{7,15},{8,0},{9,1},... | collective-permute-start | bytes 983048 | tf_op jit(solution)/shard_map/ppermute | solution.py:294
  242.5 16.4 %collective-permute-start.2 = (bf16[40,4096]{1,0:T(8,128)(2,1)S(1)}, bf16[40,4096]{1,0:T(8,128)(2,1)S(1)}, u32[]{:S(2)}, u32[]{:S(2)}) collective-permute-start(bf16[40,4096]{1,0:T(8,128)(2,1)S(1)} %get-tuple-element.79), channel_id=1, source_target_pairs={{0,16},{1,17},{2,18},{3,19},{4,20},{5,21},{6,22},{7,23},{8,24},{9,... | collective-permute-start | bytes 983048 | tf_op jit(solution)/shard_map/ppermute | solution.py:294
  243.9 16.9 %collective-permute-start.3 = (bf16[40,4096]{1,0:T(8,128)(2,1)S(1)}, bf16[40,4096]{1,0:T(8,128)(2,1)S(1)}, u32[]{:S(2)}, u32[]{:S(2)}) collective-permute-start(bf16[40,4096]{1,0:T(8,128)(2,1)S(1)} %get-tuple-element.80), channel_id=1, source_target_pairs={{0,24},{1,25},{2,26},{3,27},{4,28},{5,29},{6,30},{7,31},{8,16},{9,... | collective-permute-start | bytes 983048 | tf_op jit(solution)/shard_map/ppermute | solution.py:294
  247.2 28.7 %collective-permute-start.45 = (bf16[128,2048]{1,0:T(8,128)(2,1)S(1)}, bf16[128,2048]{1,0:T(8,128)(2,1)S(1)}, u32[]{:S(2)}, u32[]{:S(2)}) collective-permute-start(bf16[128,2048]{1,0:T(8,128)(2,1)S(1)} %get-tuple-element.125), channel_id=1, source_target_pairs={{0,1},{1,0},{2,3},{3,2},{4,5},{5,4},{6,7},{7,6},{8,9},{9,8},{10,11... | collective-permute-start | bytes 1572872 | tf_op jit(solution)/shard_map/ppermute | solution.py:304
  251.7 24.1 %collective-permute-start.46 = (bf16[128,2048]{1,0:T(8,128)(2,1)S(1)}, bf16[128,2048]{1,0:T(8,128)(2,1)S(1)}, u32[]{:S(2)}, u32[]{:S(2)}) collective-permute-start(bf16[128,2048]{1,0:T(8,128)(2,1)S(1)} %get-tuple-element.126), channel_id=1, source_target_pairs={{0,7},{1,2},{2,1},{3,4},{4,3},{5,6},{6,5},{7,0},{8,15},{9,10},{10,... | collective-permute-start | bytes 1572872 | tf_op jit(solution)/shard_map/ppermute | solution.py:304
  258.8 9.2 %collective-permute-start.14 = (bf16[72,2048]{1,0:T(8,128)(2,1)S(1)}, bf16[72,2048]{1,0:T(8,128)(2,1)S(1)}, u32[]{:S(2)}, u32[]{:S(2)}) collective-permute-start(bf16[72,2048]{1,0:T(8,128)(2,1)S(1)} %get-tuple-element.91), channel_id=1, source_target_pairs={{0,8},{1,9},{2,10},{3,11},{4,12},{5,13},{6,14},{7,15},{8,0},{9,1},... | collective-permute-start | bytes 884744 | tf_op jit(solution)/shard_map/ppermute | solution.py:294
  258.9 12.8 %collective-permute-start.15 = (bf16[72,2048]{1,0:T(8,128)(2,1)S(1)}, bf16[72,2048]{1,0:T(8,128)(2,1)S(1)}, u32[]{:S(2)}, u32[]{:S(2)}) collective-permute-start(bf16[72,2048]{1,0:T(8,128)(2,1)S(1)} %get-tuple-element.92), channel_id=1, source_target_pairs={{0,16},{1,17},{2,18},{3,19},{4,20},{5,21},{6,22},{7,23},{8,24},{9,... | collective-permute-start | bytes 884744 | tf_op jit(solution)/shard_map/ppermute | solution.py:294
  260.8 14.1 %collective-permute-start.16 = (bf16[72,2048]{1,0:T(8,128)(2,1)S(1)}, bf16[72,2048]{1,0:T(8,128)(2,1)S(1)}, u32[]{:S(2)}, u32[]{:S(2)}) collective-permute-start(bf16[72,2048]{1,0:T(8,128)(2,1)S(1)} %get-tuple-element.93), channel_id=1, source_target_pairs={{0,24},{1,25},{2,26},{3,27},{4,28},{5,29},{6,30},{7,31},{8,16},{9,... | collective-permute-start | bytes 884744 | tf_op jit(solution)/shard_map/ppermute | solution.py:294
  268.0 32.4 %collective-permute-start.4 = (bf16[40,2048]{1,0:T(8,128)(2,1)S(1)}, bf16[40,2048]{1,0:T(8,128)(2,1)S(1)}, u32[]{:S(2)}, u32[]{:S(2)}) collective-permute-start(bf16[40,2048]{1,0:T(8,128)(2,1)S(1)} %get-tuple-element.82), channel_id=1, source_target_pairs={{0,8},{1,9},{2,10},{3,11},{4,12},{5,13},{6,14},{7,15},{8,0},{9,1},... | collective-permute-start | bytes 491528 | tf_op jit(solution)/shard_map/ppermute | solution.py:294
  271.7 28.8 %collective-permute-start.5 = (bf16[40,2048]{1,0:T(8,128)(2,1)S(1)}, bf16[40,2048]{1,0:T(8,128)(2,1)S(1)}, u32[]{:S(2)}, u32[]{:S(2)}) collective-permute-start(bf16[40,2048]{1,0:T(8,128)(2,1)S(1)} %get-tuple-element.83), channel_id=1, source_target_pairs={{0,16},{1,17},{2,18},{3,19},{4,20},{5,21},{6,22},{7,23},{8,24},{9,... | collective-permute-start | bytes 491528 | tf_op jit(solution)/shard_map/ppermute | solution.py:294
  275.0 25.5 %collective-permute-start.6 = (bf16[40,2048]{1,0:T(8,128)(2,1)S(1)}, bf16[40,2048]{1,0:T(8,128)(2,1)S(1)}, u32[]{:S(2)}, u32[]{:S(2)}) collective-permute-start(bf16[40,2048]{1,0:T(8,128)(2,1)S(1)} %get-tuple-element.84), channel_id=1, source_target_pairs={{0,24},{1,25},{2,26},{3,27},{4,28},{5,29},{6,30},{7,31},{8,16},{9,... | collective-permute-start | bytes 491528 | tf_op jit(solution)/shard_map/ppermute | solution.py:294
  277.2 23.2 %collective-permute-start.47 = (bf16[128,2048]{1,0:T(8,128)(2,1)S(1)}, bf16[128,2048]{1,0:T(8,128)(2,1)S(1)}, u32[]{:S(2)}, u32[]{:S(2)}) collective-permute-start(bf16[128,2048]{1,0:T(8,128)(2,1)S(1)} %get-tuple-element.127), channel_id=1, source_target_pairs={{0,1},{1,0},{2,3},{3,2},{4,5},{5,4},{6,7},{7,6},{8,9},{9,8},{10,11... | collective-permute-start | bytes 1572872 | tf_op jit(solution)/shard_map/ppermute | solution.py:304
  281.4 19.1 %collective-permute-start.48 = (bf16[128,2048]{1,0:T(8,128)(2,1)S(1)}, bf16[128,2048]{1,0:T(8,128)(2,1)S(1)}, u32[]{:S(2)}, u32[]{:S(2)}) collective-permute-start(bf16[128,2048]{1,0:T(8,128)(2,1)S(1)} %get-tuple-element.128), channel_id=1, source_target_pairs={{0,7},{1,2},{2,1},{3,4},{4,3},{5,6},{6,5},{7,0},{8,15},{9,10},{10,... | collective-permute-start | bytes 1572872 | tf_op jit(solution)/shard_map/ppermute | solution.py:304
  (6 other events, 154.1 us)
where the time goes:
time: 304 us; the launch traced here: 302 us
  waiting for transfers between devices  166 us (55%)
  Pallas kernels  66.2 us (22%)
  starting transfers between devices  63.9 us (21%)
    ppermute x30, waiting for transfers between devices, along_x(): moved.append(lax.ppermute(parts[j], 'expert', pairs))  85.5 us
    ppermute x18, waiting for transfers between devices, along_z(): return lax.ppermute(block, 'expert', pairs)  67 us
    pallas_call x15, Pallas kernels, run(): pl.pallas_call(kernel, out_shape=outs, in_specs=specs, out_specs=[VMEM] *...  48.7 us
    ppermute x30, starting transfers between devices, along_x(): moved.append(lax.ppermute(parts[j], 'expert', pairs))  40.2 us
    ppermute x18, starting transfers between devices, along_z(): return lax.ppermute(block, 'expert', pairs)  23.7 us
    pallas_call x2, Pallas kernels, weight_grads(): pl.pallas_call(functools.partial(weight_kernel, count, turned), grid=(wid...  17.6 us
    ppermute x1, waiting for transfers between devices, per_device(): lax.ppermute(saved_inputs[0], 'pipe', [(i, sections - 1 - i) for i in ran...  13.9 us
  transfers between devices with their start and end apart: 49, of which 18 were waited for; matrix products, arithmetic and copies ran while one was open for 0% of the time, Pallas kernels for 21%

commit v1 on v0

--- a/solution.py
+++ b/solution.py
@@ -11,7 +11,6 @@
 ZN = 8
 TOK = 128
 TILE = 512
-HALF = 256
 F32 = jnp.float32
 BF16 = jnp.bfloat16
 VMEM_LIMIT = 16 * 1024 * 1024
@@ -83,7 +82,9 @@
     )
     scale = select_rows(ids_ref, meta, slot, sel_ref)
     over = width + TOK
-    shared = all(i == k and at + over == to for (i, at), (k, to) in zip(grads, ins))
+    shared = bool(ins) and all(
+        i == k and at + over == to for (i, at), (k, to) in zip(grads, ins)
+    )
 
     def move(blocks, take, put, factor):
         rows = sum(
@@ -110,7 +111,8 @@
         each_tile(2 * width // TILE, TILE, both)
     else:
         each_tile(width // TILE, TILE, lambda low: move(grads, low, low, scale))
-        each_tile(width // TILE, TILE, lambda low: move(ins, low, width + low, None))
+        if ins:
+            each_tile(width // TILE, TILE, lambda low: move(ins, low, width + low, None))
 
 
 def pick(sizes, width, ids, grads, ins):
@@ -128,13 +130,43 @@
     total = len(grads) * TOK
     *rows, sel = run(
         functools.partial(pick_kernel, sizes, width, *places),
-        [shaped(send, 2 * width)] * XN + [shaped(XN * slot, total)],
+        [shaped(send, (1 + bool(ins)) * width)] * XN + [shaped(XN * slot, total)],
         [ids, *arrays],
         4 * XN * slot * total * width,
         XN * slot * width * 8,
         smem=1,
     )
     return rows, sel
+
+
+def pick_in_kernel(sizes, width, places, sel_ref, *refs):
+    send, slot = sizes
+    refs, outs = refs[:-XN], refs[-XN:]
+
+    def step(low):
+        rows = sum(
+            jnp.dot(
+                sel_ref[:, n * TOK : (n + 1) * TOK],
+                refs[n][:, pl.ds(pl.multiple_of(at + low, TOK), TILE)],
+                preferred_element_type=F32,
+            )
+            for n, at in enumerate(places)
+        ).astype(BF16)
+        for j in range(XN):
+            outs[j][:, pl.ds(low, TILE)] = rows[j * slot : j * slot + send]
+
+    each_tile(width // TILE, TILE, step)
+
+
+def pick_ins(sizes, width, sel, ins):
+    send, slot = sizes
+    return run(
+        functools.partial(pick_in_kernel, sizes, width, tuple(at for _, at in ins)),
+        [shaped(send, width)] * XN,
+        [sel, *(array for array, _ in ins)],
+        2 * XN * slot * len(ins) * TOK * width,
+        XN * slot * width * 4,
+    )
 
 
 def stack_rows(dst, parts, sizes, base):
@@ -179,12 +211,12 @@
 
     def backward(low):
         rows = lax.dot_general(
-            pre_ref[...], w_in[pl.ds(low, HALF), :], NT, preferred_element_type=F32
+            pre_ref[...], w_in[pl.ds(low, TILE), :], NT, preferred_element_type=F32
         ).astype(BF16)
         for j in range(XN):
-            backs[j][:, pl.ds(low, HALF)] = rows[j * slot : j * slot + send]
-
-    each_tile(width // HALF, HALF, backward)
+            backs[j][:, pl.ds(low, TILE)] = rows[j * slot : j * slot + send]
+
+    each_tile(width // TILE, TILE, backward)
 
 
 def expert(sizes, got, w_in, w_out):
@@ -226,7 +258,7 @@
                 stacked[(j + 1) * slot - 16 : (j + 1) * slot, here] = jnp.zeros(
                     (16, TILE), stacked.dtype
                 )
-                stacked[j * slot : j * slot + send, here] = part[:, here]
+                stacked[j * slot : j * slot + send, here] = part[0:send, here]
             for out, (block, first) in zip(outs, outs_at):
                 if not covers(out, first, start, stop):
                     continue
@@ -339,13 +371,28 @@
         ([(a, 0), (b, 0)], [(a, over), (b, over)]) for a, b in ((near_a, near_b), (a3, b3), (a4, b4))
     ]
     blocks += [([(far_grads, 0)], [(far_ins, 0)])]
-    sels, held, returned = [], [], []
+    sels, held, kept = [], [], []
     for n, (grads, ins) in enumerate(blocks):
-        rows, sel = pick(sizes[n], width, ids, grads, ins)
+        if n == 3:
+            rows, sel = pick(sizes[n], width, ids, grads, ())
+            got_grads = along_x(rows)
+            got_ins = along_x(pick_ins(sizes[n], width, sel, ins))
+            got = [jnp.concatenate([got_grads[0], got_ins[0]], axis=1)]
+            got += [
+                jnp.concatenate(pair, axis=1) for pair in zip(got_grads[1:], got_ins[1:])
+            ]
+        else:
+            rows, sel = pick(sizes[n], width, ids, grads, ins)
+            got = along_x(rows)
         sels.append(sel)
-        *backs, x_rows, g_rows, hidden, pre = expert(sizes[n], along_x(rows), weight_in, weight_out)
+        *backs, x_rows, g_rows, hidden, pre = expert(sizes[n], got, weight_in, weight_out)
         held.append((x_rows, g_rows, hidden, pre))
-        returned.append(along_x(backs))
+        kept.append(backs)
+    cut = sizes[1][0]
+    both = along_x([jnp.concatenate(pair, axis=0) for pair in zip(kept[1], kept[0])])
+    tails = [part[cut:] for part in both[1:]]
+    returned = [[kept[0][0], *tails], [kept[1][0], *both[1:]]]
+    returned += [along_x(kept[n]) for n in (2, 3, 4)]
     xs, gs, hs, ps = zip(*held)
     grad_w_in = weight_grads(xs, ps, False)
     grad_w_out = weight_grads(gs, hs, True)

time: 304 us -> 308 us (1.013)
  waiting for transfers between devices: 166 us -> 176 us
  Pallas kernels: 66.2 us -> 61.5 us
  starting transfers between devices: 63.9 us -> 60.4 us
    ppermute x30, waiting for transfers between devices: 85.5 us -> 111 us  [along_x(): moved.append(lax.ppermute(parts[j], 'expert', pairs))]
    ppermute x18, waiting for transfers between devices: 67 us -> 50.6 us  [along_z(): return lax.ppermute(block, 'expert', pairs)]
    pallas_call x15 -> x16, Pallas kernels: 48.7 us -> 43.9 us  [run(): pl.pallas_call(kernel, out_shape=outs, in_specs=specs, out_specs=[VMEM] *...]
    unnamed x12 -> x14, local copies, waits for them, and re-layouts: 1.07 us -> 4.51 us
  transfers between devices with their start and end apart: 49 -> 49, of which waited for: 18 -> 27; matrix products, arithmetic and copies ran while one was open for 0% -> 0% of each run, Pallas kernels for 21% -> 19%
where the time goes in v1:
time: 308 us; the launch traced here: 306 us
  waiting for transfers between devices  176 us (57%)
  Pallas kernels  61.5 us (20%)
  starting transfers between devices  60.4 us (20%)
  local copies, waits for them, and re-layouts  4.7 us (2%)
    ppermute x30, waiting for transfers between devices, along_x(): moved.append(lax.ppermute(parts[j], 'expert', pairs))  111 us
    ppermute x18, waiting for transfers between devices, along_z(): return lax.ppermute(block, 'expert', pairs)  50.6 us
    pallas_call x16, Pallas kernels, run(): pl.pallas_call(kernel, out_shape=outs, in_specs=specs, out_specs=[VMEM] *...  43.9 us
    ppermute x30, starting transfers between devices, along_x(): moved.append(lax.ppermute(parts[j], 'expert', pairs))  38.9 us
    ppermute x18, starting transfers between devices, along_z(): return lax.ppermute(block, 'expert', pairs)  21.5 us
    pallas_call x2, Pallas kernels, weight_grads(): pl.pallas_call(functools.partial(weight_kernel, count, turned), grid=(wid...  17.6 us
    ppermute x1, waiting for transfers between devices, per_device(): lax.ppermute(saved_inputs[0], 'pipe', [(i, sections - 1 - i) for i in ran...  14.2 us
  transfers between devices with their start and end apart: 49, of which 27 were waited for; matrix products, arithmetic and copies ran while one was open for 0% of the time, Pallas kernels for 19%

profile of v1, /device:TPU:16, one launch (start us, length us, event | category | flops | bytes accessed | tf_op | source)
XLA Modules:
  0.0 306.3 jit_solution(7377873903036394528)
XLA Ops:
  3.1 5.9 %collective-permute-start.6 = (bf16[128,2176]{1,0:T(8,128)(2,1)S(1)}, bf16[128,2176]{1,0:T(8,128)(2,1)S(1)}, u32[]{:S(2)}, u32[]{:S(2)}) collective-permute-start(bf16[128,2176]{1,0:T(8,128)(2,1)S(1)} %fusion.1.refs_0_), channel_id=1, source_target_pairs={{0,7},{1,2},{2,1},{3,4},{4,3},{5,6},{6,5},{7,0},{8,15},{9,10},{10,... | collective-permute-start | bytes 1671176 | tf_op jit(solution)/shard_map/ppermute | solution.py:336
  9.1 14.2 %collective-permute-done.refs_1_ = bf16[128,2048]{1,0:T(8,128)(2,1)S(1)} collective-permute-done((bf16[128,2048]{1,0:T(8,128)(2,1)}, bf16[128,2048]{1,0:T(8,128)(2,1)S(1)}, u32[]{:S(2)}, u32[]{:S(2)}) %collective-permute-start) | collective-permute-done | bytes 524320 | tf_op jit(solution)/shard_map/ppermute | solution.py:360
  24.2 13.9 %collective-permute-done.7 = bf16[128,2048]{1,0:T(8,128)(2,1)S(1)} collective-permute-done((bf16[128,2048]{1,0:T(8,128)(2,1)S(1)}, bf16[128,2048]{1,0:T(8,128)(2,1)S(1)}, u32[]{:S(2)}, u32[]{:S(2)}) %collective-permute-start.7) | collective-permute-done | bytes 524320 | tf_op jit(solution)/shard_map/ppermute | solution.py:336
  41.1 22.0 %collective-permute-done.14.refs_0_ = bf16[128,4224]{1,0:T(8,128)(2,1)} collective-permute-done((bf16[128,4224]{1,0:T(8,128)(2,1)S(1)}, bf16[128,4224]{1,0:T(8,128)(2,1)}, u32[]{:S(2)}, u32[]{:S(2)}) %collective-permute-start.14) | collective-permute-done | bytes 1081376 | tf_op jit(solution)/shard_map/ppermute | solution.py:336
  67.2 2.4 shard_map.85
  73.6 3.4 %shard_map.87 = (bf16[72,4096]{1,0:T(8,128)(2,1)S(1)}, bf16[72,4096]{1,0:T(8,128)(2,1)S(1)}, bf16[72,4096]{1,0:T(8,128)(2,1)S(1)}, bf16[72,4096]{1,0:T(8,128)(2,1)S(1)}, bf16[320,256]{1,0:T(8,128)(2,1)S(1)}) custom-call(s32[1,4]{1,0:T(1,128)S(1)} %multiply_add_fusion.ids_ref, bf16[128,4224]{1,0:T(8,128)(2,1)S(1)} %copy-done.3, bf16[128,4224]{1,0:T(8,128)(2,1)S(1)} %copy-done.5), custom_call_target="tpu_custom_call" | custom-call | flops 671088640 | bytes 5242880 | tf_op jit(solution)/shard_map/pallas_call | solution.py:32
  77.0 11.5 %collective-permute-done.23.refs_1_ = bf16[128,4224]{1,0:T(8,128)(2,1)S(1)} collective-permute-done((bf16[128,4224]{1,0:T(8,128)(2,1)}, bf16[128,4224]{1,0:T(8,128)(2,1)S(1)}, u32[]{:S(2)}, u32[]{:S(2)}) %collective-permute-start.23) | collective-permute-done | bytes 1081376 | tf_op jit(solution)/shard_map/ppermute | solution.py:336
  91.4 2.1 shard_map.91
  94.8 2.8 collective-permute-start.29
  98.1 10.2 %collective-permute-done.29 = bf16[72,2048]{1,0:T(8,128)(2,1)S(1)} collective-permute-done((bf16[72,2048]{1,0:T(8,128)(2,1)S(1)}, bf16[72,2048]{1,0:T(8,128)(2,1)S(1)}, u32[]{:S(2)}, u32[]{:S(2)}) %collective-permute-start.29) | collective-permute-done | bytes 294944 | tf_op jit(solution)/shard_map/ppermute | solution.py:326
  108.3 1.8 collective-permute-start.27
  111.5 1.8 collective-permute-start.26
  115.6 2.3 shard_map.94
  120.0 6.1 %collective-permute-done.26 = bf16[72,2048]{1,0:T(8,128)(2,1)S(1)} collective-permute-done((bf16[72,2048]{1,0:T(8,128)(2,1)S(1)}, bf16[72,2048]{1,0:T(8,128)(2,1)S(1)}, u32[]{:S(2)}, u32[]{:S(2)}) %collective-permute-start.26) | collective-permute-done | bytes 294944 | tf_op jit(solution)/shard_map/ppermute | solution.py:326
  126.4 2.6 collective-permute-start.10
  129.0 4.1 %collective-permute-done.2.refs_2_ = bf16[40,4096]{1,0:T(8,128)(2,1)S(1)} collective-permute-done((bf16[40,4096]{1,0:T(8,128)(2,1)S(1)}, bf16[40,4096]{1,0:T(8,128)(2,1)S(1)}, u32[]{:S(2)}, u32[]{:S(2)}) %collective-permute-start.2) | collective-permute-done | bytes 327712 | tf_op jit(solution)/shard_map/ppermute | solution.py:326
  133.4 6.1 %collective-permute-done.25 = bf16[72,2048]{1,0:T(8,128)(2,1)S(1)} collective-permute-done((bf16[72,2048]{1,0:T(8,128)(2,1)S(1)}, bf16[72,2048]{1,0:T(8,128)(2,1)S(1)}, u32[]{:S(2)}, u32[]{:S(2)}) %collective-permute-start.25) | collective-permute-done | bytes 294944 | tf_op jit(solution)/shard_map/ppermute | solution.py:326
  140.3 5.5 %collective-permute-done.24 = bf16[72,2048]{1,0:T(8,128)(2,1)S(1)} collective-permute-done((bf16[72,2048]{1,0:T(8,128)(2,1)S(1)}, bf16[72,2048]{1,0:T(8,128)(2,1)S(1)}, u32[]{:S(2)}, u32[]{:S(2)}) %collective-permute-start.24) | collective-permute-done | bytes 294944 | tf_op jit(solution)/shard_map/ppermute | solution.py:326
  146.6 6.2 %collective-permute-done.35.refs_1_ = bf16[40,4096]{1,0:T(8,128)(2,1)S(1)} collective-permute-done((bf16[40,4096]{1,0:T(8,128)(2,1)S(1)}, bf16[40,4096]{1,0:T(8,128)(2,1)S(1)}, u32[]{:S(2)}, u32[]{:S(2)}) %collective-permute-start.35) | collective-permute-done | bytes 327712 | tf_op jit(solution)/shard_map/ppermute | solution.py:326
  153.4 27.0 %collective-permute-done.36.refs_2_ = bf16[40,4096]{1,0:T(8,128)(2,1)S(1)} collective-permute-done((bf16[40,4096]{1,0:T(8,128)(2,1)S(1)}, bf16[40,4096]{1,0:T(8,128)(2,1)S(1)}, u32[]{:S(2)}, u32[]{:S(2)}) %collective-permute-start.36) | collective-permute-done | bytes 327712 | tf_op jit(solution)/shard_map/ppermute | solution.py:326
  180.3 2.8 collective-permute-start.3
  183.1 4.7 %shard_map.93 = (bf16[72,2048]{1,0:T(8,128)(2,1)S(1)}, bf16[72,2048]{1,0:T(8,128)(2,1)S(1)}, bf16[72,2048]{1,0:T(8,128)(2,1)S(1)}, bf16[72,2048]{1,0:T(8,128)(2,...) custom-call(bf16[72,4096]{1,0:T(8,128)(2,1)S(1)} %pad_maximum_fusion, ...), custom_call_target="tpu_custom_call" | custom-call | flops 2516582400 | bytes 5242880 | tf_op jit(solution)/shard_map/pallas_call | solution.py:32
  188.0 3.7 %shard_map.95 = (bf16[40,2048]{1,0:T(8,128)(2,1)S(1)}, bf16[40,2048]{1,0:T(8,128)(2,1)S(1)}, bf16[40,2048]{1,0:T(8,128)(2,1)S(1)}, bf16[40,2048]{1,0:T(8,128)(2,...) custom-call(bf16[40,4096]{1,0:T(8,128)(2,1)S(1)} %get-tuple-element., ...), custom_call_target="tpu_custom_call" | custom-call | flops 1509949440 | bytes 3145728 | tf_op jit(solution)/shard_map/pallas_call | solution.py:32
  191.7 2.1 collective-permute-start.38
  193.8 2.8 collective-permute-start.40
  197.8 2.1 collective-permute-start.32
  199.9 4.4 %shard_map.89 = (bf16[72,4096]{1,0:T(8,128)(2,1)S(1)}, bf16[72,4096]{1,0:T(8,128)(2,1)S(1)}, bf16[72,4096]{1,0:T(8,128)(2,1)S(1)}, bf16[72,4096]{1,0:T(8,128)(2,1)S(1)}, bf16[320,256]{1,0:T(8,128)(2,1)S(1)}) custom-call(s32[1,4]{1,0:T(1,128)S(1)} %multiply_add_fusion.ids_ref, bf16[128,4224]{1,0:T(8,128)(2,1)} %collective-permute-done.14.refs_0_, ...), custom_call_target="tpu_custom_call" | custom-call | flops 671088640 | bytes 5242880 | tf_op jit(solution)/shard_map/pallas_call | solution.py:32
  204.5 2.5 collective-permute-start.17
  207.3 1.8 collective-permute-start.18
  210.7 4.7 %collective-permute-done.32.refs_3_ = bf16[72,2048]{1,0:T(8,128)(2,1)S(1)} collective-permute-done((bf16[72,2048]{1,0:T(8,128)(2,1)S(1)}, bf16[72,2048]{1,0:T(8,128)(2,1)S(1)}, u32[]{:S(2)}, u32[]{:S(2)}) %collective-permute-start.32) | collective-permute-done | bytes 294944 | tf_op jit(solution)/shard_map/ppermute | solution.py:326
  215.4 2.4 collective-permute-start.42
  217.8 3.7 %shard_map.86 = (bf16[40,2048]{1,0:T(8,128)(2,1)S(1)}, bf16[40,2048]{1,0:T(8,128)(2,1)S(1)}, bf16[40,2048]{1,0:T(8,128)(2,1)S(1)}, bf16[40,2048]{1,0:T(8,128)(2,...) custom-call(bf16[40,4096]{1,0:T(8,128)(2,1)S(1)} %get-tuple-element., ...), custom_call_target="tpu_custom_call" | custom-call | flops 1509949440 | bytes 3145728 | tf_op jit(solution)/shard_map/pallas_call | solution.py:32
  221.5 4.7 %shard_map.88 = (bf16[72,2048]{1,0:T(8,128)(2,1)S(1)}, bf16[72,2048]{1,0:T(8,128)(2,1)S(1)}, bf16[72,2048]{1,0:T(8,128)(2,1)S(1)}, bf16[72,2048]{1,0:T(8,128)(2,...) custom-call(bf16[72,4096]{1,0:T(8,128)(2,1)S(1)} %get-tuple-element., ...), custom_call_target="tpu_custom_call" | custom-call | flops 2516582400 | bytes 5242880 | tf_op jit(solution)/shard_map/pallas_call | solution.py:32
  229.1 2.5 collective-permute-done.17.refs_2_
  231.6 5.4 %collective-permute-done.18.refs_3_ = bf16[72,4096]{1,0:T(8,128)(2,1)S(1)} collective-permute-done((bf16[72,4096]{1,0:T(8,128)(2,1)S(1)}, bf16[72,4096]{1,0:T(8,128)(2,1)S(1)}, u32[]{:S(2)}, u32[]{:S(2)}) %collective-permute-start.18) | collective-permute-done | bytes 589856 | tf_op jit(solution)/shard_map/ppermute | solution.py:326
  237.0 4.8 %shard_map.90 = (bf16[72,2048]{1,0:T(8,128)(2,1)S(1)}, bf16[72,2048]{1,0:T(8,128)(2,1)S(1)}, bf16[72,2048]{1,0:T(8,128)(2,1)S(1)}, bf16[72,2048]{1,0:T(8,128)(2,...) custom-call(bf16[72,4096]{1,0:T(8,128)(2,1)S(1)} %get-tuple-element., ...), custom_call_target="tpu_custom_call" | custom-call | flops 2516582400 | bytes 5242880 | tf_op jit(solution)/shard_map/pallas_call | solution.py:32
  242.0 3.2 %collective-permute-start.20 = (bf16[72,2048]{1,0:T(8,128)(2,1)S(1)}, bf16[72,2048]{1,0:T(8,128)(2,1)S(1)}, u32[]{:S(2)}, u32[]{:S(2)}) collective-permute-start(bf16[72,2048]{1,0:T(8,128)(2,1)S(1)} %get-tuple-element.105), channel_id=1, source_target_pairs={{0,16},{1,17},{2,18},{3,19},{4,20},{5,21},{6,22},{7,23},{8,24},{9,... | collective-permute-start | bytes 884744 | tf_op jit(solution)/shard_map/ppermute | solution.py:326
  246.6 4.1 %collective-permute-done.19.refs_1_ = bf16[72,2048]{1,0:T(8,128)(2,1)S(1)} collective-permute-done((bf16[72,2048]{1,0:T(8,128)(2,1)S(1)}, bf16[72,2048]{1,0:T(8,128)(2,1)S(1)}, u32[]{:S(2)}, u32[]{:S(2)}) %collective-permute-start.19) | collective-permute-done | bytes 294944 | tf_op jit(solution)/shard_map/ppermute | solution.py:326
  250.7 2.0 collective-permute-start.13
  252.7 2.8 collective-permute-done.20.refs_2_
  256.0 13.9 %collective-permute-done.21.refs_3_ = bf16[72,2048]{1,0:T(8,128)(2,1)S(1)} collective-permute-done((bf16[72,2048]{1,0:T(8,128)(2,1)S(1)}, bf16[72,2048]{1,0:T(8,128)(2,1)S(1)}, u32[]{:S(2)}, u32[]{:S(2)}) %collective-permute-start.21) | collective-permute-done | bytes 294944 | tf_op jit(solution)/shard_map/ppermute | solution.py:326
  271.8 2.2 collective-permute-start.46
  274.1 3.5 %collective-permute-done.13.refs_3_ = bf16[112,2048]{1,0:T(8,128)(2,1)S(1)} collective-permute-done((bf16[112,2048]{1,0:T(8,128)(2,1)S(1)}, bf16[112,2048]{1,0:T(8,128)(2,1)S(1)}, u32[]{:S(2)}, u32[]{:S(2)}) %collective-permute-start.13) | collective-permute-done | bytes 458784 | tf_op jit(solution)/shard_map/ppermute | solution.py:326
  277.7 4.9 %collective-permute-done.11.refs_1_ = bf16[112,2048]{1,0:T(8,128)(2,1)S(1)} collective-permute-done((bf16[112,2048]{1,0:T(8,128)(2,1)S(1)}, bf16[112,2048]{1,0:T(8,128)(2,1)S(1)}, u32[]{:S(2)}, u32[]{:S(2)}) %collective-permute-start.11) | collective-permute-done | bytes 458784 | tf_op jit(solution)/shard_map/ppermute | solution.py:326
  284.5 2.3 collective-permute-start.48
  286.9 7.8 %shard_map.102 = bf16[384,2048]{1,0:T(8,128)(2,1)} custom-call(bf16[192,2048]{1,0:T(8,128)(2,1)S(1)} %get-tuple-element.147.refs_0_, bf16[320,2048]{1,0:T(8,128)(2,1)S(1)} %get-tuple-element.148.refs_1_, bf16[320,2048]{1,0:T(8,128)(2,1)S(1)} %get-tuple-element.149.refs_2_, bf16[320,2048]{1,0:T(8,128)(2,1)S(1)} %get-tuple-element.150.refs_3_, ...), custom_call_target="tpu_custom_call" | custom-call | flops 2113929216 | bytes 5505024 | tf_op jit(solution)/shard_map/pallas_call | solution.py:306
  294.7 9.7 %shard_map.101 = bf16[2048,768]{1,0:T(8,128)(2,1)} custom-call(bf16[192,2048]{1,0:T(8,128)(2,1)S(1)} %get-tuple-element.137.refs_0_, bf16[320,2048]{1,0:T(8,128)(2,1)S(1)} %get-tuple-element.138.refs_1_, bf16[320,2048]{1,0:T(8,128)(2,1)S(1)} %get-tuple-element.139.refs_2_, bf16[320,2048]{1,0:T(8,128)(2,1)S(1)} %get-tuple-element.140.refs_3_, ...), custom_call_target="tpu_custom_call" | custom-call | flops 4227858432 | bytes 5505024 | tf_op jit(solution)/shard_map/pallas_call | solution.py:306
  304.4 1.8 shard_map.100
  (101 shorter events, 39.9 us)
Async XLA Ops:
  3.1 20.5 %collective-permute-start.6 = (bf16[128,2176]{1,0:T(8,128)(2,1)S(1)}, bf16[128,2176]{1,0:T(8,128)(2,1)S(1)}, u32[]{:S(2)}, u32[]{:S(2)}) collective-permute-start(bf16[128,2176]{1,0:T(8,128)(2,1)S(1)} %fusion.1.refs_0_), channel_id=1, source_target_pairs={{0,7},{1,2},{2,1},{3,4},{4,3},{5,6},{6,5},{7,0},{8,15},{9,10},{10,... | collective-permute-start | bytes 1671176 | tf_op jit(solution)/shard_map/ppermute | solution.py:336
  9.1 14.2 %collective-permute-start = (bf16[128,2048]{1,0:T(8,128)(2,1)}, bf16[128,2048]{1,0:T(8,128)(2,1)S(1)}, u32[]{:S(2)}, u32[]{:S(2)}) collective-permute-start(bf16[128,2048]{1,0:T(8,128)(2,1)} %bitcast.31), channel_id=1, source_target_pairs={{0,224},{32,192},{64,160},{96,128},{128,96},{160,64},{192,32},{224... | collective-permute-start | bytes 1572872 | tf_op jit(solution)/shard_map/ppermute | solution.py:360
  9.1 15.1 %collective-permute-start.4 = (bf16[128,2176]{1,0:T(8,128)(2,1)S(1)}, bf16[128,2176]{1,0:T(8,128)(2,1)S(1)}, u32[]{:S(2)}, u32[]{:S(2)}) collective-permute-start(bf16[128,2176]{1,0:T(8,128)(2,1)S(1)} %fusion.1.refs_0_), channel_id=1, source_target_pairs={{0,1},{1,0},{2,3},{3,2},{4,5},{5,4},{6,7},{7,6},{8,9},{9,8},{10,11... | collective-permute-start | bytes 1671176 | tf_op jit(solution)/shard_map/ppermute | solution.py:336
  23.2 14.9 %collective-permute-start.7 = (bf16[128,2048]{1,0:T(8,128)(2,1)S(1)}, bf16[128,2048]{1,0:T(8,128)(2,1)S(1)}, u32[]{:S(2)}, u32[]{:S(2)}) collective-permute-start(bf16[128,2048]{1,0:T(8,128)(2,1)S(1)} %collective-permute-done.refs_1_), channel_id=1, source_target_pairs={{0,7},{1,2},{2,1},{3,4},{4,3},{5,6},{6,5},{7,0},{8,15},{9,10},{10,... | collective-permute-start | bytes 1572872 | tf_op jit(solution)/shard_map/ppermute | solution.py:336
  23.6 15.7 %collective-permute-start.5 = (bf16[128,2048]{1,0:T(8,128)(2,1)S(1)}, bf16[128,2048]{1,0:T(8,128)(2,1)S(1)}, u32[]{:S(2)}, u32[]{:S(2)}) collective-permute-start(bf16[128,2048]{1,0:T(8,128)(2,1)S(1)} %collective-permute-done.refs_1_), channel_id=1, source_target_pairs={{0,1},{1,0},{2,3},{3,2},{4,5},{5,4},{6,7},{7,6},{8,9},{9,8},{10,11... | collective-permute-start | bytes 1572872 | tf_op jit(solution)/shard_map/ppermute | solution.py:336
  38.1 24.9 %collective-permute-start.14 = (bf16[128,4224]{1,0:T(8,128)(2,1)S(1)}, bf16[128,4224]{1,0:T(8,128)(2,1)}, u32[]{:S(2)}, u32[]{:S(2)}) collective-permute-start(bf16[128,4224]{1,0:T(8,128)(2,1)S(1)} %constant_dynamic-update-slice_fusion.2.refs_1_), channel_id=1, source_target_pairs={{0,1},{1,0},{2,3},{3,2},{4,5},{5,4},{6,7},{7,6},{8,9},{9,8},{10,11... | collective-permute-start | bytes 3244040 | tf_op jit(solution)/shard_map/ppermute | solution.py:336
  39.3 26.2 %collective-permute-start.15 = (bf16[128,4224]{1,0:T(8,128)(2,1)S(1)}, bf16[128,4224]{1,0:T(8,128)(2,1)}, u32[]{:S(2)}, u32[]{:S(2)}) collective-permute-start(bf16[128,4224]{1,0:T(8,128)(2,1)S(1)} %constant_dynamic-update-slice_fusion.refs_0_), channel_id=1, source_target_pairs={{0,7},{1,2},{2,1},{3,4},{4,3},{5,6},{6,5},{7,0},{8,15},{9,10},{10,... | collective-permute-start | bytes 3244040 | tf_op jit(solution)/shard_map/ppermute | solution.py:336
  63.1 25.4 %collective-permute-start.23 = (bf16[128,4224]{1,0:T(8,128)(2,1)}, bf16[128,4224]{1,0:T(8,128)(2,1)S(1)}, u32[]{:S(2)}, u32[]{:S(2)}) collective-permute-start(bf16[128,4224]{1,0:T(8,128)(2,1)} %collective-permute-done.14.refs_0_), channel_id=1, source_target_pairs={{0,7},{1,2},{2,1},{3,4},{4,3},{5,6},{6,5},{7,0},{8,15},{9,10},{10,... | collective-permute-start | bytes 3244040 | tf_op jit(solution)/shard_map/ppermute | solution.py:336
  65.5 24.8 %collective-permute-start.22 = (bf16[128,4224]{1,0:T(8,128)(2,1)}, bf16[128,4224]{1,0:T(8,128)(2,1)S(1)}, u32[]{:S(2)}, u32[]{:S(2)}) collective-permute-start(bf16[128,4224]{1,0:T(8,128)(2,1)} %collective-permute-done.15.refs_1_), channel_id=1, source_target_pairs={{0,1},{1,0},{2,3},{3,2},{4,5},{5,4},{6,7},{7,6},{8,9},{9,8},{10,11... | collective-permute-start | bytes 3244040 | tf_op jit(solution)/shard_map/ppermute | solution.py:336
  69.6 56.8 %collective-permute-start.1 = (bf16[40,4096]{1,0:T(8,128)(2,1)S(1)}, bf16[40,4096]{1,0:T(8,128)(2,1)S(1)}, u32[]{:S(2)}, u32[]{:S(2)}) collective-permute-start(bf16[40,4096]{1,0:T(8,128)(2,1)S(1)} %get-tuple-element.82), channel_id=1, source_target_pairs={{0,8},{1,9},{2,10},{3,11},{4,12},{5,13},{6,14},{7,15},{8,0},{9,1},... | collective-permute-start | bytes 983048 | tf_op jit(solution)/shard_map/ppermute | solution.py:326
  88.5 26.6 %collective-permute-start.33 = (bf16[128,2176]{1,0:T(8,128)(2,1)S(1)}, bf16[128,2176]{1,0:T(8,128)(2,1)S(1)}, u32[]{:S(2)}, u32[]{:S(2)}) collective-permute-start(bf16[128,2176]{1,0:T(8,128)(2,1)S(1)} %slice.23), channel_id=1, source_target_pairs={{0,1},{1,0},{2,3},{3,2},{4,5},{5,4},{6,7},{7,6},{8,9},{9,8},{10,11... | collective-permute-start | bytes 1671176 | tf_op jit(solution)/shard_map/ppermute | solution.py:336
  90.3 23.0 %collective-permute-start.34 = (bf16[128,2048]{1,0:T(8,128)(2,1)S(1)}, bf16[128,2048]{1,0:T(8,128)(2,1)S(1)}, u32[]{:S(2)}, u32[]{:S(2)}) collective-permute-start(bf16[128,2048]{1,0:T(8,128)(2,1)S(1)} %slice.24), channel_id=1, source_target_pairs={{0,7},{1,2},{2,1},{3,4},{4,3},{5,6},{6,5},{7,0},{8,15},{9,10},{10,... | collective-permute-start | bytes 1572872 | tf_op jit(solution)/shard_map/ppermute | solution.py:336
  94.8 13.5 %collective-permute-start.29 = (bf16[72,2048]{1,0:T(8,128)(2,1)S(1)}, bf16[72,2048]{1,0:T(8,128)(2,1)S(1)}, u32[]{:S(2)}, u32[]{:S(2)}) collective-permute-start(bf16[72,2048]{1,0:T(8,128)(2,1)S(1)} %get-tuple-element.115), channel_id=1, source_target_pairs={{0,24},{1,25},{2,26},{3,27},{4,28},{5,29},{6,30},{7,31},{8,16},{9,... | collective-permute-start | bytes 884744 | tf_op jit(solution)/shard_map/ppermute | solution.py:326
  97.6 13.9 %collective-permute-start.28 = (bf16[72,2048]{1,0:T(8,128)(2,1)S(1)}, bf16[72,2048]{1,0:T(8,128)(2,1)S(1)}, u32[]{:S(2)}, u32[]{:S(2)}) collective-permute-start(bf16[72,2048]{1,0:T(8,128)(2,1)S(1)} %get-tuple-element.114), channel_id=1, source_target_pairs={{0,24},{1,25},{2,26},{3,27},{4,28},{5,29},{6,30},{7,31},{8,16},{9,... | collective-permute-start | bytes 884744 | tf_op jit(solution)/shard_map/ppermute | solution.py:326
  108.3 11.4 %collective-permute-start.27 = (bf16[72,2048]{1,0:T(8,128)(2,1)S(1)}, bf16[72,2048]{1,0:T(8,128)(2,1)S(1)}, u32[]{:S(2)}, u32[]{:S(2)}) collective-permute-start(bf16[72,2048]{1,0:T(8,128)(2,1)S(1)} %get-tuple-element.113), channel_id=1, source_target_pairs={{0,16},{1,17},{2,18},{3,19},{4,20},{5,21},{6,22},{7,23},{8,24},{9,... | collective-permute-start | bytes 884744 | tf_op jit(solution)/shard_map/ppermute | solution.py:326
  111.5 14.6 %collective-permute-start.26 = (bf16[72,2048]{1,0:T(8,128)(2,1)S(1)}, bf16[72,2048]{1,0:T(8,128)(2,1)S(1)}, u32[]{:S(2)}, u32[]{:S(2)}) collective-permute-start(bf16[72,2048]{1,0:T(8,128)(2,1)S(1)} %get-tuple-element.112), channel_id=1, source_target_pairs={{0,16},{1,17},{2,18},{3,19},{4,20},{5,21},{6,22},{7,23},{8,24},{9,... | collective-permute-start | bytes 884744 | tf_op jit(solution)/shard_map/ppermute | solution.py:326
  113.4 19.7 %collective-permute-start.2 = (bf16[40,4096]{1,0:T(8,128)(2,1)S(1)}, bf16[40,4096]{1,0:T(8,128)(2,1)S(1)}, u32[]{:S(2)}, u32[]{:S(2)}) collective-permute-start(bf16[40,4096]{1,0:T(8,128)(2,1)S(1)} %get-tuple-element.83), channel_id=1, source_target_pairs={{0,16},{1,17},{2,18},{3,19},{4,20},{5,21},{6,22},{7,23},{8,24},{9,... | collective-permute-start | bytes 983048 | tf_op jit(solution)/shard_map/ppermute | solution.py:326
  115.2 24.4 %collective-permute-start.25 = (bf16[72,2048]{1,0:T(8,128)(2,1)S(1)}, bf16[72,2048]{1,0:T(8,128)(2,1)S(1)}, u32[]{:S(2)}, u32[]{:S(2)}) collective-permute-start(bf16[72,2048]{1,0:T(8,128)(2,1)S(1)} %get-tuple-element.111), channel_id=1, source_target_pairs={{0,8},{1,9},{2,10},{3,11},{4,12},{5,13},{6,14},{7,15},{8,0},{9,1},... | collective-permute-start | bytes 884744 | tf_op jit(solution)/shard_map/ppermute | solution.py:326
  119.7 26.1 %collective-permute-start.24 = (bf16[72,2048]{1,0:T(8,128)(2,1)S(1)}, bf16[72,2048]{1,0:T(8,128)(2,1)S(1)}, u32[]{:S(2)}, u32[]{:S(2)}) collective-permute-start(bf16[72,2048]{1,0:T(8,128)(2,1)S(1)} %get-tuple-element.110), channel_id=1, source_target_pairs={{0,8},{1,9},{2,10},{3,11},{4,12},{5,13},{6,14},{7,15},{8,0},{9,1},... | collective-permute-start | bytes 884744 | tf_op jit(solution)/shard_map/ppermute | solution.py:326
  126.1 26.8 %collective-permute-start.35 = (bf16[40,4096]{1,0:T(8,128)(2,1)S(1)}, bf16[40,4096]{1,0:T(8,128)(2,1)S(1)}, u32[]{:S(2)}, u32[]{:S(2)}) collective-permute-start(bf16[40,4096]{1,0:T(8,128)(2,1)S(1)} %get-tuple-element.122), channel_id=1, source_target_pairs={{0,8},{1,9},{2,10},{3,11},{4,12},{5,13},{6,14},{7,15},{8,0},{9,1},... | collective-permute-start | bytes 983048 | tf_op jit(solution)/shard_map/ppermute | solution.py:326
  126.4 67.3 %collective-permute-start.10 = (bf16[72,4096]{1,0:T(8,128)(2,1)S(1)}, bf16[72,4096]{1,0:T(8,128)(2,1)S(1)}, u32[]{:S(2)}, u32[]{:S(2)}) collective-permute-start(bf16[72,4096]{1,0:T(8,128)(2,1)S(1)} %get-tuple-element.89), channel_id=1, source_target_pairs={{0,24},{1,25},{2,26},{3,27},{4,28},{5,29},{6,30},{7,31},{8,16},{9,... | collective-permute-start | bytes 1769480 | tf_op jit(solution)/shard_map/ppermute | solution.py:326
  133.1 60.7 %collective-permute-start.8 = (bf16[72,4096]{1,0:T(8,128)(2,1)S(1)}, bf16[72,4096]{1,0:T(8,128)(2,1)S(1)}, u32[]{:S(2)}, u32[]{:S(2)}) collective-permute-start(bf16[72,4096]{1,0:T(8,128)(2,1)S(1)} %get-tuple-element.87), channel_id=1, source_target_pairs={{0,8},{1,9},{2,10},{3,11},{4,12},{5,13},{6,14},{7,15},{8,0},{9,1},... | collective-permute-start | bytes 1769480 | tf_op jit(solution)/shard_map/ppermute | solution.py:326
  139.5 57.0 %collective-permute-start.9 = (bf16[72,4096]{1,0:T(8,128)(2,1)S(1)}, bf16[72,4096]{1,0:T(8,128)(2,1)S(1)}, u32[]{:S(2)}, u32[]{:S(2)}) collective-permute-start(bf16[72,4096]{1,0:T(8,128)(2,1)S(1)} %get-tuple-element.88), channel_id=1, source_target_pairs={{0,16},{1,17},{2,18},{3,19},{4,20},{5,21},{6,22},{7,23},{8,24},{9,... | collective-permute-start | bytes 1769480 | tf_op jit(solution)/shard_map/ppermute | solution.py:326
  145.8 34.5 %collective-permute-start.36 = (bf16[40,4096]{1,0:T(8,128)(2,1)S(1)}, bf16[40,4096]{1,0:T(8,128)(2,1)S(1)}, u32[]{:S(2)}, u32[]{:S(2)}) collective-permute-start(bf16[40,4096]{1,0:T(8,128)(2,1)S(1)} %get-tuple-element.123), channel_id=1, source_target_pairs={{0,16},{1,17},{2,18},{3,19},{4,20},{5,21},{6,22},{7,23},{8,24},{9,... | collective-permute-start | bytes 983048 | tf_op jit(solution)/shard_map/ppermute | solution.py:326
  152.8 35.0 %collective-permute-start.37 = (bf16[40,4096]{1,0:T(8,128)(2,1)S(1)}, bf16[40,4096]{1,0:T(8,128)(2,1)S(1)}, u32[]{:S(2)}, u32[]{:S(2)}) collective-permute-start(bf16[40,4096]{1,0:T(8,128)(2,1)S(1)} %get-tuple-element.124), channel_id=1, source_target_pairs={{0,24},{1,25},{2,26},{3,27},{4,28},{5,29},{6,30},{7,31},{8,16},{9,... | collective-permute-start | bytes 983048 | tf_op jit(solution)/shard_map/ppermute | solution.py:326
  180.3 11.3 %collective-permute-start.3 = (bf16[40,4096]{1,0:T(8,128)(2,1)S(1)}, bf16[40,4096]{1,0:T(8,128)(2,1)S(1)}, u32[]{:S(2)}, u32[]{:S(2)}) collective-permute-start(bf16[40,4096]{1,0:T(8,128)(2,1)S(1)} %get-tuple-element.84), channel_id=1, source_target_pairs={{0,24},{1,25},{2,26},{3,27},{4,28},{5,29},{6,30},{7,31},{8,16},{9,... | collective-permute-start | bytes 983048 | tf_op jit(solution)/shard_map/ppermute | solution.py:326
  187.9 10.0 %collective-permute-start.30 = (bf16[72,2048]{1,0:T(8,128)(2,1)S(1)}, bf16[72,2048]{1,0:T(8,128)(2,1)S(1)}, u32[]{:S(2)}, u32[]{:S(2)}) collective-permute-start(bf16[72,2048]{1,0:T(8,128)(2,1)S(1)} %get-tuple-element.117), channel_id=1, source_target_pairs={{0,8},{1,9},{2,10},{3,11},{4,12},{5,13},{6,14},{7,15},{8,0},{9,1},... | collective-permute-start | bytes 884744 | tf_op jit(solution)/shard_map/ppermute | solution.py:326
  191.7 12.6 %collective-permute-start.38 = (bf16[40,2048]{1,0:T(8,128)(2,1)S(1)}, bf16[40,2048]{1,0:T(8,128)(2,1)S(1)}, u32[]{:S(2)}, u32[]{:S(2)}) collective-permute-start(bf16[40,2048]{1,0:T(8,128)(2,1)S(1)} %get-tuple-element.126), channel_id=1, source_target_pairs={{0,8},{1,9},{2,10},{3,11},{4,12},{5,13},{6,14},{7,15},{8,0},{9,1},... | collective-permute-start | bytes 491528 | tf_op jit(solution)/shard_map/ppermute | solution.py:326
  193.8 10.8 %collective-permute-start.39 = (bf16[40,2048]{1,0:T(8,128)(2,1)S(1)}, bf16[40,2048]{1,0:T(8,128)(2,1)S(1)}, u32[]{:S(2)}, u32[]{:S(2)}) collective-permute-start(bf16[40,2048]{1,0:T(8,128)(2,1)S(1)} %get-tuple-element.127), channel_id=1, source_target_pairs={{0,16},{1,17},{2,18},{3,19},{4,20},{5,21},{6,22},{7,23},{8,24},{9,... | collective-permute-start | bytes 491528 | tf_op jit(solution)/shard_map/ppermute | solution.py:326
  193.8 13.5 %collective-permute-start.40 = (bf16[40,2048]{1,0:T(8,128)(2,1)S(1)}, bf16[40,2048]{1,0:T(8,128)(2,1)S(1)}, u32[]{:S(2)}, u32[]{:S(2)}) collective-permute-start(bf16[40,2048]{1,0:T(8,128)(2,1)S(1)} %get-tuple-element.128), channel_id=1, source_target_pairs={{0,24},{1,25},{2,26},{3,27},{4,28},{5,29},{6,30},{7,31},{8,16},{9,... | collective-permute-start | bytes 491528 | tf_op jit(solution)/shard_map/ppermute | solution.py:326
  196.5 13.7 %collective-permute-start.31 = (bf16[72,2048]{1,0:T(8,128)(2,1)S(1)}, bf16[72,2048]{1,0:T(8,128)(2,1)S(1)}, u32[]{:S(2)}, u32[]{:S(2)}) collective-permute-start(bf16[72,2048]{1,0:T(8,128)(2,1)S(1)} %get-tuple-element.118), channel_id=1, source_target_pairs={{0,16},{1,17},{2,18},{3,19},{4,20},{5,21},{6,22},{7,23},{8,24},{9,... | collective-permute-start | bytes 884744 | tf_op jit(solution)/shard_map/ppermute | solution.py:326
  197.8 17.6 %collective-permute-start.32 = (bf16[72,2048]{1,0:T(8,128)(2,1)S(1)}, bf16[72,2048]{1,0:T(8,128)(2,1)S(1)}, u32[]{:S(2)}, u32[]{:S(2)}) collective-permute-start(bf16[72,2048]{1,0:T(8,128)(2,1)S(1)} %get-tuple-element.119), channel_id=1, source_target_pairs={{0,24},{1,25},{2,26},{3,27},{4,28},{5,29},{6,30},{7,31},{8,16},{9,... | collective-permute-start | bytes 884744 | tf_op jit(solution)/shard_map/ppermute | solution.py:326
  204.3 24.8 %collective-permute-start.16 = (bf16[72,4096]{1,0:T(8,128)(2,1)S(1)}, bf16[72,4096]{1,0:T(8,128)(2,1)S(1)}, u32[]{:S(2)}, u32[]{:S(2)}) collective-permute-start(bf16[72,4096]{1,0:T(8,128)(2,1)S(1)} %get-tuple-element.100), channel_id=1, source_target_pairs={{0,8},{1,9},{2,10},{3,11},{4,12},{5,13},{6,14},{7,15},{8,0},{9,1},... | collective-permute-start | bytes 1769480 | tf_op jit(solution)/shard_map/ppermute | solution.py:326
  204.5 27.0 %collective-permute-start.17 = (bf16[72,4096]{1,0:T(8,128)(2,1)S(1)}, bf16[72,4096]{1,0:T(8,128)(2,1)S(1)}, u32[]{:S(2)}, u32[]{:S(2)}) collective-permute-start(bf16[72,4096]{1,0:T(8,128)(2,1)S(1)} %get-tuple-element.101), channel_id=1, source_target_pairs={{0,16},{1,17},{2,18},{3,19},{4,20},{5,21},{6,22},{7,23},{8,24},{9,... | collective-permute-start | bytes 1769480 | tf_op jit(solution)/shard_map/ppermute | solution.py:326
  207.3 29.7 %collective-permute-start.18 = (bf16[72,4096]{1,0:T(8,128)(2,1)S(1)}, bf16[72,4096]{1,0:T(8,128)(2,1)S(1)}, u32[]{:S(2)}, u32[]{:S(2)}) collective-permute-start(bf16[72,4096]{1,0:T(8,128)(2,1)S(1)} %get-tuple-element.102), channel_id=1, source_target_pairs={{0,24},{1,25},{2,26},{3,27},{4,28},{5,29},{6,30},{7,31},{8,16},{9,... | collective-permute-start | bytes 1769480 | tf_op jit(solution)/shard_map/ppermute | solution.py:326
  210.2 15.9 %collective-permute-start.41 = (bf16[128,1024]{1,0:T(8,128)(2,1)S(1)}, bf16[128,1024]{1,0:T(8,128)(2,1)S(1)}, u32[]{:S(2)}, u32[]{:S(2)}) collective-permute-start(bf16[128,1024]{1,0:T(8,128)(2,1)S(1)} %get-tuple-element.129), channel_id=1, source_target_pairs={{0,1},{1,0},{2,3},{3,2},{4,5},{5,4},{6,7},{7,6},{8,9},{9,8},{10,11... | collective-permute-start | bytes 786440 | tf_op jit(solution)/shard_map/ppermute | solution.py:336
  215.4 10.8 %collective-permute-start.42 = (bf16[128,1024]{1,0:T(8,128)(2,1)S(1)}, bf16[128,1024]{1,0:T(8,128)(2,1)S(1)}, u32[]{:S(2)}, u32[]{:S(2)}) collective-permute-start(bf16[128,1024]{1,0:T(8,128)(2,1)S(1)} %get-tuple-element.130), channel_id=1, source_target_pairs={{0,7},{1,2},{2,1},{3,4},{4,3},{5,6},{6,5},{7,0},{8,15},{9,10},{10,... | collective-permute-start | bytes 786440 | tf_op jit(solution)/shard_map/ppermute | solution.py:336
  227.5 42.4 %collective-permute-start.43 = (bf16[128,2048]{1,0:T(8,128)(2,1)S(1)}, bf16[128,2048]{1,0:T(8,128)(2,1)S(1)}, u32[]{:S(2)}, u32[]{:S(2)}) collective-permute-start(bf16[128,2048]{1,0:T(8,128)(2,1)S(1)} %get-tuple-element.131), channel_id=1, source_target_pairs={{0,1},{1,0},{2,3},{3,2},{4,5},{5,4},{6,7},{7,6},{8,9},{9,8},{10,11... | collective-permute-start | bytes 1572872 | tf_op jit(solution)/shard_map/ppermute | solution.py:336
  227.6 42.3 %collective-permute-start.44 = (bf16[128,2048]{1,0:T(8,128)(2,1)S(1)}, bf16[128,2048]{1,0:T(8,128)(2,1)S(1)}, u32[]{:S(2)}, u32[]{:S(2)}) collective-permute-start(bf16[128,2048]{1,0:T(8,128)(2,1)S(1)} %get-tuple-element.132), channel_id=1, source_target_pairs={{0,7},{1,2},{2,1},{3,4},{4,3},{5,6},{6,5},{7,0},{8,15},{9,10},{10,... | collective-permute-start | bytes 1572872 | tf_op jit(solution)/shard_map/ppermute | solution.py:336
  241.7 8.9 %collective-permute-start.19 = (bf16[72,2048]{1,0:T(8,128)(2,1)S(1)}, bf16[72,2048]{1,0:T(8,128)(2,1)S(1)}, u32[]{:S(2)}, u32[]{:S(2)}) collective-permute-start(bf16[72,2048]{1,0:T(8,128)(2,1)S(1)} %get-tuple-element.104), channel_id=1, source_target_pairs={{0,8},{1,9},{2,10},{3,11},{4,12},{5,13},{6,14},{7,15},{8,0},{9,1},... | collective-permute-start | bytes 884744 | tf_op jit(solution)/shard_map/ppermute | solution.py:326
  242.0 13.5 %collective-permute-start.20 = (bf16[72,2048]{1,0:T(8,128)(2,1)S(1)}, bf16[72,2048]{1,0:T(8,128)(2,1)S(1)}, u32[]{:S(2)}, u32[]{:S(2)}) collective-permute-start(bf16[72,2048]{1,0:T(8,128)(2,1)S(1)} %get-tuple-element.105), channel_id=1, source_target_pairs={{0,16},{1,17},{2,18},{3,19},{4,20},{5,21},{6,22},{7,23},{8,24},{9,... | collective-permute-start | bytes 884744 | tf_op jit(solution)/shard_map/ppermute | solution.py:326
  245.2 24.7 %collective-permute-start.21 = (bf16[72,2048]{1,0:T(8,128)(2,1)S(1)}, bf16[72,2048]{1,0:T(8,128)(2,1)S(1)}, u32[]{:S(2)}, u32[]{:S(2)}) collective-permute-start(bf16[72,2048]{1,0:T(8,128)(2,1)S(1)} %get-tuple-element.106), channel_id=1, source_target_pairs={{0,24},{1,25},{2,26},{3,27},{4,28},{5,29},{6,30},{7,31},{8,16},{9,... | collective-permute-start | bytes 884744 | tf_op jit(solution)/shard_map/ppermute | solution.py:326
  250.7 26.9 %collective-permute-start.13 = (bf16[112,2048]{1,0:T(8,128)(2,1)S(1)}, bf16[112,2048]{1,0:T(8,128)(2,1)S(1)}, u32[]{:S(2)}, u32[]{:S(2)}) collective-permute-start(bf16[112,2048]{1,0:T(8,128)(2,1)S(1)} %pad_maximum_fusion.6), channel_id=1, source_target_pairs={{0,24},{1,25},{2,26},{3,27},{4,28},{5,29},{6,30},{7,31},{8,16},{9,... | collective-permute-start | bytes 1376264 | tf_op jit(solution)/shard_map/ppermute | solution.py:326
  255.5 22.1 %collective-permute-start.12 = (bf16[112,2048]{1,0:T(8,128)(2,1)S(1)}, bf16[112,2048]{1,0:T(8,128)(2,1)S(1)}, u32[]{:S(2)}, u32[]{:S(2)}) collective-permute-start(bf16[112,2048]{1,0:T(8,128)(2,1)S(1)} %pad_maximum_fusion.5), channel_id=1, source_target_pairs={{0,16},{1,17},{2,18},{3,19},{4,20},{5,21},{6,22},{7,23},{8,24},{9,... | collective-permute-start | bytes 1376264 | tf_op jit(solution)/shard_map/ppermute | solution.py:326
  271.2 11.4 %collective-permute-start.45 = (bf16[128,2048]{1,0:T(8,128)(2,1)S(1)}, bf16[128,2048]{1,0:T(8,128)(2,1)S(1)}, u32[]{:S(2)}, u32[]{:S(2)}) collective-permute-start(bf16[128,2048]{1,0:T(8,128)(2,1)S(1)} %get-tuple-element.133), channel_id=1, source_target_pairs={{0,1},{1,0},{2,3},{3,2},{4,5},{5,4},{6,7},{7,6},{8,9},{9,8},{10,11... | collective-permute-start | bytes 1572872 | tf_op jit(solution)/shard_map/ppermute | solution.py:336
  271.8 10.8 %collective-permute-start.46 = (bf16[128,2048]{1,0:T(8,128)(2,1)S(1)}, bf16[128,2048]{1,0:T(8,128)(2,1)S(1)}, u32[]{:S(2)}, u32[]{:S(2)}) collective-permute-start(bf16[128,2048]{1,0:T(8,128)(2,1)S(1)} %get-tuple-element.134), channel_id=1, source_target_pairs={{0,7},{1,2},{2,1},{3,4},{4,3},{5,6},{6,5},{7,0},{8,15},{9,10},{10,... | collective-permute-start | bytes 1572872 | tf_op jit(solution)/shard_map/ppermute | solution.py:336
  284.0 20.5 %collective-permute-start.47 = (bf16[128,2048]{1,0:T(8,128)(2,1)S(1)}, bf16[128,2048]{1,0:T(8,128)(2,1)S(1)}, u32[]{:S(2)}, u32[]{:S(2)}) collective-permute-start(bf16[128,2048]{1,0:T(8,128)(2,1)S(1)} %get-tuple-element.135), channel_id=1, source_target_pairs={{0,1},{1,0},{2,3},{3,2},{4,5},{5,4},{6,7},{7,6},{8,9},{9,8},{10,11... | collective-permute-start | bytes 1572872 | tf_op jit(solution)/shard_map/ppermute | solution.py:336
  284.5 19.9 %collective-permute-start.48 = (bf16[128,2048]{1,0:T(8,128)(2,1)S(1)}, bf16[128,2048]{1,0:T(8,128)(2,1)S(1)}, u32[]{:S(2)}, u32[]{:S(2)}) collective-permute-start(bf16[128,2048]{1,0:T(8,128)(2,1)S(1)} %get-tuple-element.136), channel_id=1, source_target_pairs={{0,7},{1,2},{2,1},{3,4},{4,3},{5,6},{6,5},{7,0},{8,15},{9,10},{10,... | collective-permute-start | bytes 1572872 | tf_op jit(solution)/shard_map/ppermute | solution.py:336
  (7 other events, 165.5 us)

commit v2 on v1

--- a/solution.py
+++ b/solution.py
@@ -11,6 +11,7 @@
 ZN = 8
 TOK = 128
 TILE = 512
+WIDE = 1024
 F32 = jnp.float32
 BF16 = jnp.bfloat16
 VMEM_LIMIT = 16 * 1024 * 1024
@@ -245,18 +246,19 @@
         return first <= start and stop <= first + ref.shape[1]
 
     def columns(first, low):
-        return pl.ds(pl.multiple_of(low - first, TOK), TILE)
+        return pl.ds(pl.multiple_of(low - first, TOK), tile)
 
     whole = all(r.shape[1] == width for r in (*incoming, *outs))
+    tile = WIDE if whole and len(outs) == 2 else TILE
     spans = [(0, width)] if whole else [(0, width // 2), (width // 2, width)]
     for start, stop in spans:
 
         def step(offset):
             low = pl.multiple_of(start + offset, TOK)
-            here = pl.ds(low, TILE)
+            here = pl.ds(low, tile)
             for j, part in enumerate(backs):
                 stacked[(j + 1) * slot - 16 : (j + 1) * slot, here] = jnp.zeros(
-                    (16, TILE), stacked.dtype
+                    (16, tile), stacked.dtype
                 )
                 stacked[j * slot : j * slot + send, here] = part[0:send, here]
             for out, (block, first) in zip(outs, outs_at):
@@ -273,7 +275,7 @@
                         total = total + ref[:, columns(begin, low)].astype(F32)
                 out[:, columns(first, low)] = total.astype(out.dtype)
 
-        each_tile((stop - start) // TILE, TILE, step)
+        each_tile((stop - start) // tile, tile, step)
 
 
 def combine(sizes, sel, backs, incoming, adds, outs_at, outs):

time: 308 us -> 307 us (level)
  no operation moved by 1% of the time
where the time goes in v2:
time: 307 us; the launch traced here: 306 us
  waiting for transfers between devices  176 us (57%)
  Pallas kernels  60.7 us (20%)
  starting transfers between devices  60.4 us (20%)
  local copies, waits for them, and re-layouts  4.7 us (2%)
    ppermute x30, waiting for transfers between devices, along_x(): moved.append(lax.ppermute(parts[j], 'expert', pairs))  111 us
    ppermute x18, waiting for transfers between devices, along_z(): return lax.ppermute(block, 'expert', pairs)  50.6 us
    pallas_call x16, Pallas kernels, run(): pl.pallas_call(kernel, out_shape=outs, in_specs=specs, out_specs=[VMEM] *...  43.2 us
    ppermute x30, starting transfers between devices, along_x(): moved.append(lax.ppermute(parts[j], 'expert', pairs))  38.9 us
    ppermute x18, starting transfers between devices, along_z(): return lax.ppermute(block, 'expert', pairs)  21.5 us
    pallas_call x2, Pallas kernels, weight_grads(): pl.pallas_call(functools.partial(weight_kernel, count, turned), grid=(wid...  17.6 us
    ppermute x1, waiting for transfers between devices, per_device(): lax.ppermute(saved_inputs[0], 'pipe', [(i, sections - 1 - i) for i in ran...  14.2 us
  transfers between devices with their start and end apart: 49, of which 27 were waited for; matrix products, arithmetic and copies ran while one was open for 0% of the time, Pallas kernels for 19%

profile of v2, /device:TPU:16, one launch (start us, length us, event | category | flops | bytes accessed | tf_op | source)
XLA Modules:
  0.0 305.5 jit_solution(3517436596852778372)
XLA Ops:
  3.1 5.9 %collective-permute-start.6 = (bf16[128,2176]{1,0:T(8,128)(2,1)S(1)}, bf16[128,2176]{1,0:T(8,128)(2,1)S(1)}, u32[]{:S(2)}, u32[]{:S(2)}) collective-permute-start(bf16[128,2176]{1,0:T(8,128)(2,1)S(1)} %fusion.1.refs_0_), channel_id=1, source_target_pairs={{0,7},{1,2},{2,1},{3,4},{4,3},{5,6},{6,5},{7,0},{8,15},{9,10},{10,... | collective-permute-start | bytes 1671176 | tf_op jit(solution)/shard_map/ppermute | solution.py:338
  9.1 14.2 %collective-permute-done.refs_1_ = bf16[128,2048]{1,0:T(8,128)(2,1)S(1)} collective-permute-done((bf16[128,2048]{1,0:T(8,128)(2,1)}, bf16[128,2048]{1,0:T(8,128)(2,1)S(1)}, u32[]{:S(2)}, u32[]{:S(2)}) %collective-permute-start) | collective-permute-done | bytes 524320 | tf_op jit(solution)/shard_map/ppermute | solution.py:362
  24.2 13.9 %collective-permute-done.7 = bf16[128,2048]{1,0:T(8,128)(2,1)S(1)} collective-permute-done((bf16[128,2048]{1,0:T(8,128)(2,1)S(1)}, bf16[128,2048]{1,0:T(8,128)(2,1)S(1)}, u32[]{:S(2)}, u32[]{:S(2)}) %collective-permute-start.7) | collective-permute-done | bytes 524320 | tf_op jit(solution)/shard_map/ppermute | solution.py:338
  41.1 22.0 %collective-permute-done.14.refs_0_ = bf16[128,4224]{1,0:T(8,128)(2,1)} collective-permute-done((bf16[128,4224]{1,0:T(8,128)(2,1)S(1)}, bf16[128,4224]{1,0:T(8,128)(2,1)}, u32[]{:S(2)}, u32[]{:S(2)}) %collective-permute-start.14) | collective-permute-done | bytes 1081376 | tf_op jit(solution)/shard_map/ppermute | solution.py:338
  67.2 2.4 shard_map.85
  73.6 3.4 %shard_map.87 = (bf16[72,4096]{1,0:T(8,128)(2,1)S(1)}, bf16[72,4096]{1,0:T(8,128)(2,1)S(1)}, bf16[72,4096]{1,0:T(8,128)(2,1)S(1)}, bf16[72,4096]{1,0:T(8,128)(2,1)S(1)}, bf16[320,256]{1,0:T(8,128)(2,1)S(1)}) custom-call(s32[1,4]{1,0:T(1,128)S(1)} %multiply_add_fusion.ids_ref, bf16[128,4224]{1,0:T(8,128)(2,1)S(1)} %copy-done.3, bf16[128,4224]{1,0:T(8,128)(2,1)S(1)} %copy-done.5), custom_call_target="tpu_custom_call" | custom-call | flops 671088640 | bytes 5242880 | tf_op jit(solution)/shard_map/pallas_call | solution.py:33
  77.0 11.5 %collective-permute-done.23.refs_1_ = bf16[128,4224]{1,0:T(8,128)(2,1)S(1)} collective-permute-done((bf16[128,4224]{1,0:T(8,128)(2,1)}, bf16[128,4224]{1,0:T(8,128)(2,1)S(1)}, u32[]{:S(2)}, u32[]{:S(2)}) %collective-permute-start.23) | collective-permute-done | bytes 1081376 | tf_op jit(solution)/shard_map/ppermute | solution.py:338
  91.4 2.1 shard_map.91
  94.8 2.8 collective-permute-start.29
  98.1 10.2 %collective-permute-done.29 = bf16[72,2048]{1,0:T(8,128)(2,1)S(1)} collective-permute-done((bf16[72,2048]{1,0:T(8,128)(2,1)S(1)}, bf16[72,2048]{1,0:T(8,128)(2,1)S(1)}, u32[]{:S(2)}, u32[]{:S(2)}) %collective-permute-start.29) | collective-permute-done | bytes 294944 | tf_op jit(solution)/shard_map/ppermute | solution.py:328
  108.3 1.8 collective-permute-start.27
  111.5 1.8 collective-permute-start.26
  115.6 2.3 shard_map.94
  120.0 6.1 %collective-permute-done.26 = bf16[72,2048]{1,0:T(8,128)(2,1)S(1)} collective-permute-done((bf16[72,2048]{1,0:T(8,128)(2,1)S(1)}, bf16[72,2048]{1,0:T(8,128)(2,1)S(1)}, u32[]{:S(2)}, u32[]{:S(2)}) %collective-permute-start.26) | collective-permute-done | bytes 294944 | tf_op jit(solution)/shard_map/ppermute | solution.py:328
  126.4 2.6 collective-permute-start.10
  129.0 4.1 %collective-permute-done.2.refs_2_ = bf16[40,4096]{1,0:T(8,128)(2,1)S(1)} collective-permute-done((bf16[40,4096]{1,0:T(8,128)(2,1)S(1)}, bf16[40,4096]{1,0:T(8,128)(2,1)S(1)}, u32[]{:S(2)}, u32[]{:S(2)}) %collective-permute-start.2) | collective-permute-done | bytes 327712 | tf_op jit(solution)/shard_map/ppermute | solution.py:328
  133.4 6.1 %collective-permute-done.25 = bf16[72,2048]{1,0:T(8,128)(2,1)S(1)} collective-permute-done((bf16[72,2048]{1,0:T(8,128)(2,1)S(1)}, bf16[72,2048]{1,0:T(8,128)(2,1)S(1)}, u32[]{:S(2)}, u32[]{:S(2)}) %collective-permute-start.25) | collective-permute-done | bytes 294944 | tf_op jit(solution)/shard_map/ppermute | solution.py:328
  140.3 5.5 %collective-permute-done.24 = bf16[72,2048]{1,0:T(8,128)(2,1)S(1)} collective-permute-done((bf16[72,2048]{1,0:T(8,128)(2,1)S(1)}, bf16[72,2048]{1,0:T(8,128)(2,1)S(1)}, u32[]{:S(2)}, u32[]{:S(2)}) %collective-permute-start.24) | collective-permute-done | bytes 294944 | tf_op jit(solution)/shard_map/ppermute | solution.py:328
  146.6 6.2 %collective-permute-done.35.refs_1_ = bf16[40,4096]{1,0:T(8,128)(2,1)S(1)} collective-permute-done((bf16[40,4096]{1,0:T(8,128)(2,1)S(1)}, bf16[40,4096]{1,0:T(8,128)(2,1)S(1)}, u32[]{:S(2)}, u32[]{:S(2)}) %collective-permute-start.35) | collective-permute-done | bytes 327712 | tf_op jit(solution)/shard_map/ppermute | solution.py:328
  153.4 27.0 %collective-permute-done.36.refs_2_ = bf16[40,4096]{1,0:T(8,128)(2,1)S(1)} collective-permute-done((bf16[40,4096]{1,0:T(8,128)(2,1)S(1)}, bf16[40,4096]{1,0:T(8,128)(2,1)S(1)}, u32[]{:S(2)}, u32[]{:S(2)}) %collective-permute-start.36) | collective-permute-done | bytes 327712 | tf_op jit(solution)/shard_map/ppermute | solution.py:328
  180.3 2.8 collective-permute-start.3
  183.1 4.7 %shard_map.93 = (bf16[72,2048]{1,0:T(8,128)(2,1)S(1)}, bf16[72,2048]{1,0:T(8,128)(2,1)S(1)}, bf16[72,2048]{1,0:T(8,128)(2,1)S(1)}, bf16[72,2048]{1,0:T(8,128)(2,...) custom-call(bf16[72,4096]{1,0:T(8,128)(2,1)S(1)} %pad_maximum_fusion, ...), custom_call_target="tpu_custom_call" | custom-call | flops 2516582400 | bytes 5242880 | tf_op jit(solution)/shard_map/pallas_call | solution.py:33
  188.0 3.7 %shard_map.95 = (bf16[40,2048]{1,0:T(8,128)(2,1)S(1)}, bf16[40,2048]{1,0:T(8,128)(2,1)S(1)}, bf16[40,2048]{1,0:T(8,128)(2,1)S(1)}, bf16[40,2048]{1,0:T(8,128)(2,...) custom-call(bf16[40,4096]{1,0:T(8,128)(2,1)S(1)} %get-tuple-element., ...), custom_call_target="tpu_custom_call" | custom-call | flops 1509949440 | bytes 3145728 | tf_op jit(solution)/shard_map/pallas_call | solution.py:33
  191.7 2.1 collective-permute-start.38
  193.8 2.8 collective-permute-start.40
  197.8 2.1 collective-permute-start.32
  199.9 4.4 %shard_map.89 = (bf16[72,4096]{1,0:T(8,128)(2,1)S(1)}, bf16[72,4096]{1,0:T(8,128)(2,1)S(1)}, bf16[72,4096]{1,0:T(8,128)(2,1)S(1)}, bf16[72,4096]{1,0:T(8,128)(2,1)S(1)}, bf16[320,256]{1,0:T(8,128)(2,1)S(1)}) custom-call(s32[1,4]{1,0:T(1,128)S(1)} %multiply_add_fusion.ids_ref, bf16[128,4224]{1,0:T(8,128)(2,1)} %collective-permute-done.14.refs_0_, ...), custom_call_target="tpu_custom_call" | custom-call | flops 671088640 | bytes 5242880 | tf_op jit(solution)/shard_map/pallas_call | solution.py:33
  204.5 2.5 collective-permute-start.17
  207.3 1.8 collective-permute-start.18
  210.7 4.7 %collective-permute-done.32.refs_3_ = bf16[72,2048]{1,0:T(8,128)(2,1)S(1)} collective-permute-done((bf16[72,2048]{1,0:T(8,128)(2,1)S(1)}, bf16[72,2048]{1,0:T(8,128)(2,1)S(1)}, u32[]{:S(2)}, u32[]{:S(2)}) %collective-permute-start.32) | collective-permute-done | bytes 294944 | tf_op jit(solution)/shard_map/ppermute | solution.py:328
  215.4 2.4 collective-permute-start.42
  217.8 3.7 %shard_map.86 = (bf16[40,2048]{1,0:T(8,128)(2,1)S(1)}, bf16[40,2048]{1,0:T(8,128)(2,1)S(1)}, bf16[40,2048]{1,0:T(8,128)(2,1)S(1)}, bf16[40,2048]{1,0:T(8,128)(2,...) custom-call(bf16[40,4096]{1,0:T(8,128)(2,1)S(1)} %get-tuple-element., ...), custom_call_target="tpu_custom_call" | custom-call | flops 1509949440 | bytes 3145728 | tf_op jit(solution)/shard_map/pallas_call | solution.py:33
  221.5 4.7 %shard_map.88 = (bf16[72,2048]{1,0:T(8,128)(2,1)S(1)}, bf16[72,2048]{1,0:T(8,128)(2,1)S(1)}, bf16[72,2048]{1,0:T(8,128)(2,1)S(1)}, bf16[72,2048]{1,0:T(8,128)(2,...) custom-call(bf16[72,4096]{1,0:T(8,128)(2,1)S(1)} %get-tuple-element., ...), custom_call_target="tpu_custom_call" | custom-call | flops 2516582400 | bytes 5242880 | tf_op jit(solution)/shard_map/pallas_call | solution.py:33
  229.1 2.5 collective-permute-done.17.refs_2_
  231.6 5.4 %collective-permute-done.18.refs_3_ = bf16[72,4096]{1,0:T(8,128)(2,1)S(1)} collective-permute-done((bf16[72,4096]{1,0:T(8,128)(2,1)S(1)}, bf16[72,4096]{1,0:T(8,128)(2,1)S(1)}, u32[]{:S(2)}, u32[]{:S(2)}) %collective-permute-start.18) | collective-permute-done | bytes 589856 | tf_op jit(solution)/shard_map/ppermute | solution.py:328
  237.0 4.8 %shard_map.90 = (bf16[72,2048]{1,0:T(8,128)(2,1)S(1)}, bf16[72,2048]{1,0:T(8,128)(2,1)S(1)}, bf16[72,2048]{1,0:T(8,128)(2,1)S(1)}, bf16[72,2048]{1,0:T(8,128)(2,...) custom-call(bf16[72,4096]{1,0:T(8,128)(2,1)S(1)} %get-tuple-element., ...), custom_call_target="tpu_custom_call" | custom-call | flops 2516582400 | bytes 5242880 | tf_op jit(solution)/shard_map/pallas_call | solution.py:33
  242.0 3.2 %collective-permute-start.20 = (bf16[72,2048]{1,0:T(8,128)(2,1)S(1)}, bf16[72,2048]{1,0:T(8,128)(2,1)S(1)}, u32[]{:S(2)}, u32[]{:S(2)}) collective-permute-start(bf16[72,2048]{1,0:T(8,128)(2,1)S(1)} %get-tuple-element.105), channel_id=1, source_target_pairs={{0,16},{1,17},{2,18},{3,19},{4,20},{5,21},{6,22},{7,23},{8,24},{9,... | collective-permute-start | bytes 884744 | tf_op jit(solution)/shard_map/ppermute | solution.py:328
  246.6 4.1 %collective-permute-done.19.refs_1_ = bf16[72,2048]{1,0:T(8,128)(2,1)S(1)} collective-permute-done((bf16[72,2048]{1,0:T(8,128)(2,1)S(1)}, bf16[72,2048]{1,0:T(8,128)(2,1)S(1)}, u32[]{:S(2)}, u32[]{:S(2)}) %collective-permute-start.19) | collective-permute-done | bytes 294944 | tf_op jit(solution)/shard_map/ppermute | solution.py:328
  250.7 2.0 collective-permute-start.13
  252.7 2.8 collective-permute-done.20.refs_2_
  256.0 13.9 %collective-permute-done.21.refs_3_ = bf16[72,2048]{1,0:T(8,128)(2,1)S(1)} collective-permute-done((bf16[72,2048]{1,0:T(8,128)(2,1)S(1)}, bf16[72,2048]{1,0:T(8,128)(2,1)S(1)}, u32[]{:S(2)}, u32[]{:S(2)}) %collective-permute-start.21) | collective-permute-done | bytes 294944 | tf_op jit(solution)/shard_map/ppermute | solution.py:328
  271.4 2.2 collective-permute-start.46
  273.8 3.9 %collective-permute-done.13.refs_3_ = bf16[112,2048]{1,0:T(8,128)(2,1)S(1)} collective-permute-done((bf16[112,2048]{1,0:T(8,128)(2,1)S(1)}, bf16[112,2048]{1,0:T(8,128)(2,1)S(1)}, u32[]{:S(2)}, u32[]{:S(2)}) %collective-permute-start.13) | collective-permute-done | bytes 458784 | tf_op jit(solution)/shard_map/ppermute | solution.py:328
  277.7 4.6 %collective-permute-done.11.refs_1_ = bf16[112,2048]{1,0:T(8,128)(2,1)S(1)} collective-permute-done((bf16[112,2048]{1,0:T(8,128)(2,1)S(1)}, bf16[112,2048]{1,0:T(8,128)(2,1)S(1)}, u32[]{:S(2)}, u32[]{:S(2)}) %collective-permute-start.11) | collective-permute-done | bytes 458784 | tf_op jit(solution)/shard_map/ppermute | solution.py:328
  283.8 2.4 collective-permute-start.48
  286.1 7.8 %shard_map.102 = bf16[384,2048]{1,0:T(8,128)(2,1)} custom-call(bf16[192,2048]{1,0:T(8,128)(2,1)S(1)} %get-tuple-element.147.refs_0_, bf16[320,2048]{1,0:T(8,128)(2,1)S(1)} %get-tuple-element.148.refs_1_, bf16[320,2048]{1,0:T(8,128)(2,1)S(1)} %get-tuple-element.149.refs_2_, bf16[320,2048]{1,0:T(8,128)(2,1)S(1)} %get-tuple-element.150.refs_3_, ...), custom_call_target="tpu_custom_call" | custom-call | flops 2113929216 | bytes 5505024 | tf_op jit(solution)/shard_map/pallas_call | solution.py:308
  294.0 9.7 %shard_map.101 = bf16[2048,768]{1,0:T(8,128)(2,1)} custom-call(bf16[192,2048]{1,0:T(8,128)(2,1)S(1)} %get-tuple-element.137.refs_0_, bf16[320,2048]{1,0:T(8,128)(2,1)S(1)} %get-tuple-element.138.refs_1_, bf16[320,2048]{1,0:T(8,128)(2,1)S(1)} %get-tuple-element.139.refs_2_, bf16[320,2048]{1,0:T(8,128)(2,1)S(1)} %get-tuple-element.140.refs_3_, ...), custom_call_target="tpu_custom_call" | custom-call | flops 4227858432 | bytes 5505024 | tf_op jit(solution)/shard_map/pallas_call | solution.py:308
  303.7 1.8 shard_map.100
  (101 shorter events, 39.2 us)
Async XLA Ops:
  3.1 20.5 %collective-permute-start.6 = (bf16[128,2176]{1,0:T(8,128)(2,1)S(1)}, bf16[128,2176]{1,0:T(8,128)(2,1)S(1)}, u32[]{:S(2)}, u32[]{:S(2)}) collective-permute-start(bf16[128,2176]{1,0:T(8,128)(2,1)S(1)} %fusion.1.refs_0_), channel_id=1, source_target_pairs={{0,7},{1,2},{2,1},{3,4},{4,3},{5,6},{6,5},{7,0},{8,15},{9,10},{10,... | collective-permute-start | bytes 1671176 | tf_op jit(solution)/shard_map/ppermute | solution.py:338
  9.1 14.2 %collective-permute-start = (bf16[128,2048]{1,0:T(8,128)(2,1)}, bf16[128,2048]{1,0:T(8,128)(2,1)S(1)}, u32[]{:S(2)}, u32[]{:S(2)}) collective-permute-start(bf16[128,2048]{1,0:T(8,128)(2,1)} %bitcast.31), channel_id=1, source_target_pairs={{0,224},{32,192},{64,160},{96,128},{128,96},{160,64},{192,32},{224... | collective-permute-start | bytes 1572872 | tf_op jit(solution)/shard_map/ppermute | solution.py:362
  9.1 15.1 %collective-permute-start.4 = (bf16[128,2176]{1,0:T(8,128)(2,1)S(1)}, bf16[128,2176]{1,0:T(8,128)(2,1)S(1)}, u32[]{:S(2)}, u32[]{:S(2)}) collective-permute-start(bf16[128,2176]{1,0:T(8,128)(2,1)S(1)} %fusion.1.refs_0_), channel_id=1, source_target_pairs={{0,1},{1,0},{2,3},{3,2},{4,5},{5,4},{6,7},{7,6},{8,9},{9,8},{10,11... | collective-permute-start | bytes 1671176 | tf_op jit(solution)/shard_map/ppermute | solution.py:338
  23.2 14.9 %collective-permute-start.7 = (bf16[128,2048]{1,0:T(8,128)(2,1)S(1)}, bf16[128,2048]{1,0:T(8,128)(2,1)S(1)}, u32[]{:S(2)}, u32[]{:S(2)}) collective-permute-start(bf16[128,2048]{1,0:T(8,128)(2,1)S(1)} %collective-permute-done.refs_1_), channel_id=1, source_target_pairs={{0,7},{1,2},{2,1},{3,4},{4,3},{5,6},{6,5},{7,0},{8,15},{9,10},{10,... | collective-permute-start | bytes 1572872 | tf_op jit(solution)/shard_map/ppermute | solution.py:338
  23.6 15.7 %collective-permute-start.5 = (bf16[128,2048]{1,0:T(8,128)(2,1)S(1)}, bf16[128,2048]{1,0:T(8,128)(2,1)S(1)}, u32[]{:S(2)}, u32[]{:S(2)}) collective-permute-start(bf16[128,2048]{1,0:T(8,128)(2,1)S(1)} %collective-permute-done.refs_1_), channel_id=1, source_target_pairs={{0,1},{1,0},{2,3},{3,2},{4,5},{5,4},{6,7},{7,6},{8,9},{9,8},{10,11... | collective-permute-start | bytes 1572872 | tf_op jit(solution)/shard_map/ppermute | solution.py:338
  38.1 24.9 %collective-permute-start.14 = (bf16[128,4224]{1,0:T(8,128)(2,1)S(1)}, bf16[128,4224]{1,0:T(8,128)(2,1)}, u32[]{:S(2)}, u32[]{:S(2)}) collective-permute-start(bf16[128,4224]{1,0:T(8,128)(2,1)S(1)} %constant_dynamic-update-slice_fusion.2.refs_1_), channel_id=1, source_target_pairs={{0,1},{1,0},{2,3},{3,2},{4,5},{5,4},{6,7},{7,6},{8,9},{9,8},{10,11... | collective-permute-start | bytes 3244040 | tf_op jit(solution)/shard_map/ppermute | solution.py:338
  39.3 26.2 %collective-permute-start.15 = (bf16[128,4224]{1,0:T(8,128)(2,1)S(1)}, bf16[128,4224]{1,0:T(8,128)(2,1)}, u32[]{:S(2)}, u32[]{:S(2)}) collective-permute-start(bf16[128,4224]{1,0:T(8,128)(2,1)S(1)} %constant_dynamic-update-slice_fusion.refs_0_), channel_id=1, source_target_pairs={{0,7},{1,2},{2,1},{3,4},{4,3},{5,6},{6,5},{7,0},{8,15},{9,10},{10,... | collective-permute-start | bytes 3244040 | tf_op jit(solution)/shard_map/ppermute | solution.py:338
  63.1 25.4 %collective-permute-start.23 = (bf16[128,4224]{1,0:T(8,128)(2,1)}, bf16[128,4224]{1,0:T(8,128)(2,1)S(1)}, u32[]{:S(2)}, u32[]{:S(2)}) collective-permute-start(bf16[128,4224]{1,0:T(8,128)(2,1)} %collective-permute-done.14.refs_0_), channel_id=1, source_target_pairs={{0,7},{1,2},{2,1},{3,4},{4,3},{5,6},{6,5},{7,0},{8,15},{9,10},{10,... | collective-permute-start | bytes 3244040 | tf_op jit(solution)/shard_map/ppermute | solution.py:338
  65.5 24.8 %collective-permute-start.22 = (bf16[128,4224]{1,0:T(8,128)(2,1)}, bf16[128,4224]{1,0:T(8,128)(2,1)S(1)}, u32[]{:S(2)}, u32[]{:S(2)}) collective-permute-start(bf16[128,4224]{1,0:T(8,128)(2,1)} %collective-permute-done.15.refs_1_), channel_id=1, source_target_pairs={{0,1},{1,0},{2,3},{3,2},{4,5},{5,4},{6,7},{7,6},{8,9},{9,8},{10,11... | collective-permute-start | bytes 3244040 | tf_op jit(solution)/shard_map/ppermute | solution.py:338
  69.6 56.8 %collective-permute-start.1 = (bf16[40,4096]{1,0:T(8,128)(2,1)S(1)}, bf16[40,4096]{1,0:T(8,128)(2,1)S(1)}, u32[]{:S(2)}, u32[]{:S(2)}) collective-permute-start(bf16[40,4096]{1,0:T(8,128)(2,1)S(1)} %get-tuple-element.82), channel_id=1, source_target_pairs={{0,8},{1,9},{2,10},{3,11},{4,12},{5,13},{6,14},{7,15},{8,0},{9,1},... | collective-permute-start | bytes 983048 | tf_op jit(solution)/shard_map/ppermute | solution.py:328
  88.5 26.6 %collective-permute-start.33 = (bf16[128,2176]{1,0:T(8,128)(2,1)S(1)}, bf16[128,2176]{1,0:T(8,128)(2,1)S(1)}, u32[]{:S(2)}, u32[]{:S(2)}) collective-permute-start(bf16[128,2176]{1,0:T(8,128)(2,1)S(1)} %slice.23), channel_id=1, source_target_pairs={{0,1},{1,0},{2,3},{3,2},{4,5},{5,4},{6,7},{7,6},{8,9},{9,8},{10,11... | collective-permute-start | bytes 1671176 | tf_op jit(solution)/shard_map/ppermute | solution.py:338
  90.3 23.0 %collective-permute-start.34 = (bf16[128,2048]{1,0:T(8,128)(2,1)S(1)}, bf16[128,2048]{1,0:T(8,128)(2,1)S(1)}, u32[]{:S(2)}, u32[]{:S(2)}) collective-permute-start(bf16[128,2048]{1,0:T(8,128)(2,1)S(1)} %slice.24), channel_id=1, source_target_pairs={{0,7},{1,2},{2,1},{3,4},{4,3},{5,6},{6,5},{7,0},{8,15},{9,10},{10,... | collective-permute-start | bytes 1572872 | tf_op jit(solution)/shard_map/ppermute | solution.py:338
  94.8 13.5 %collective-permute-start.29 = (bf16[72,2048]{1,0:T(8,128)(2,1)S(1)}, bf16[72,2048]{1,0:T(8,128)(2,1)S(1)}, u32[]{:S(2)}, u32[]{:S(2)}) collective-permute-start(bf16[72,2048]{1,0:T(8,128)(2,1)S(1)} %get-tuple-element.115), channel_id=1, source_target_pairs={{0,24},{1,25},{2,26},{3,27},{4,28},{5,29},{6,30},{7,31},{8,16},{9,... | collective-permute-start | bytes 884744 | tf_op jit(solution)/shard_map/ppermute | solution.py:328
  97.6 13.9 %collective-permute-start.28 = (bf16[72,2048]{1,0:T(8,128)(2,1)S(1)}, bf16[72,2048]{1,0:T(8,128)(2,1)S(1)}, u32[]{:S(2)}, u32[]{:S(2)}) collective-permute-start(bf16[72,2048]{1,0:T(8,128)(2,1)S(1)} %get-tuple-element.114), channel_id=1, source_target_pairs={{0,24},{1,25},{2,26},{3,27},{4,28},{5,29},{6,30},{7,31},{8,16},{9,... | collective-permute-start | bytes 884744 | tf_op jit(solution)/shard_map/ppermute | solution.py:328
  108.3 11.4 %collective-permute-start.27 = (bf16[72,2048]{1,0:T(8,128)(2,1)S(1)}, bf16[72,2048]{1,0:T(8,128)(2,1)S(1)}, u32[]{:S(2)}, u32[]{:S(2)}) collective-permute-start(bf16[72,2048]{1,0:T(8,128)(2,1)S(1)} %get-tuple-element.113), channel_id=1, source_target_pairs={{0,16},{1,17},{2,18},{3,19},{4,20},{5,21},{6,22},{7,23},{8,24},{9,... | collective-permute-start | bytes 884744 | tf_op jit(solution)/shard_map/ppermute | solution.py:328
  111.5 14.6 %collective-permute-start.26 = (bf16[72,2048]{1,0:T(8,128)(2,1)S(1)}, bf16[72,2048]{1,0:T(8,128)(2,1)S(1)}, u32[]{:S(2)}, u32[]{:S(2)}) collective-permute-start(bf16[72,2048]{1,0:T(8,128)(2,1)S(1)} %get-tuple-element.112), channel_id=1, source_target_pairs={{0,16},{1,17},{2,18},{3,19},{4,20},{5,21},{6,22},{7,23},{8,24},{9,... | collective-permute-start | bytes 884744 | tf_op jit(solution)/shard_map/ppermute | solution.py:328
  113.4 19.7 %collective-permute-start.2 = (bf16[40,4096]{1,0:T(8,128)(2,1)S(1)}, bf16[40,4096]{1,0:T(8,128)(2,1)S(1)}, u32[]{:S(2)}, u32[]{:S(2)}) collective-permute-start(bf16[40,4096]{1,0:T(8,128)(2,1)S(1)} %get-tuple-element.83), channel_id=1, source_target_pairs={{0,16},{1,17},{2,18},{3,19},{4,20},{5,21},{6,22},{7,23},{8,24},{9,... | collective-permute-start | bytes 983048 | tf_op jit(solution)/shard_map/ppermute | solution.py:328
  115.2 24.4 %collective-permute-start.25 = (bf16[72,2048]{1,0:T(8,128)(2,1)S(1)}, bf16[72,2048]{1,0:T(8,128)(2,1)S(1)}, u32[]{:S(2)}, u32[]{:S(2)}) collective-permute-start(bf16[72,2048]{1,0:T(8,128)(2,1)S(1)} %get-tuple-element.111), channel_id=1, source_target_pairs={{0,8},{1,9},{2,10},{3,11},{4,12},{5,13},{6,14},{7,15},{8,0},{9,1},... | collective-permute-start | bytes 884744 | tf_op jit(solution)/shard_map/ppermute | solution.py:328
  119.7 26.1 %collective-permute-start.24 = (bf16[72,2048]{1,0:T(8,128)(2,1)S(1)}, bf16[72,2048]{1,0:T(8,128)(2,1)S(1)}, u32[]{:S(2)}, u32[]{:S(2)}) collective-permute-start(bf16[72,2048]{1,0:T(8,128)(2,1)S(1)} %get-tuple-element.110), channel_id=1, source_target_pairs={{0,8},{1,9},{2,10},{3,11},{4,12},{5,13},{6,14},{7,15},{8,0},{9,1},... | collective-permute-start | bytes 884744 | tf_op jit(solution)/shard_map/ppermute | solution.py:328
  126.1 26.8 %collective-permute-start.35 = (bf16[40,4096]{1,0:T(8,128)(2,1)S(1)}, bf16[40,4096]{1,0:T(8,128)(2,1)S(1)}, u32[]{:S(2)}, u32[]{:S(2)}) collective-permute-start(bf16[40,4096]{1,0:T(8,128)(2,1)S(1)} %get-tuple-element.122), channel_id=1, source_target_pairs={{0,8},{1,9},{2,10},{3,11},{4,12},{5,13},{6,14},{7,15},{8,0},{9,1},... | collective-permute-start | bytes 983048 | tf_op jit(solution)/shard_map/ppermute | solution.py:328
  126.4 67.3 %collective-permute-start.10 = (bf16[72,4096]{1,0:T(8,128)(2,1)S(1)}, bf16[72,4096]{1,0:T(8,128)(2,1)S(1)}, u32[]{:S(2)}, u32[]{:S(2)}) collective-permute-start(bf16[72,4096]{1,0:T(8,128)(2,1)S(1)} %get-tuple-element.89), channel_id=1, source_target_pairs={{0,24},{1,25},{2,26},{3,27},{4,28},{5,29},{6,30},{7,31},{8,16},{9,... | collective-permute-start | bytes 1769480 | tf_op jit(solution)/shard_map/ppermute | solution.py:328
  133.1 60.7 %collective-permute-start.8 = (bf16[72,4096]{1,0:T(8,128)(2,1)S(1)}, bf16[72,4096]{1,0:T(8,128)(2,1)S(1)}, u32[]{:S(2)}, u32[]{:S(2)}) collective-permute-start(bf16[72,4096]{1,0:T(8,128)(2,1)S(1)} %get-tuple-element.87), channel_id=1, source_target_pairs={{0,8},{1,9},{2,10},{3,11},{4,12},{5,13},{6,14},{7,15},{8,0},{9,1},... | collective-permute-start | bytes 1769480 | tf_op jit(solution)/shard_map/ppermute | solution.py:328
  139.5 57.0 %collective-permute-start.9 = (bf16[72,4096]{1,0:T(8,128)(2,1)S(1)}, bf16[72,4096]{1,0:T(8,128)(2,1)S(1)}, u32[]{:S(2)}, u32[]{:S(2)}) collective-permute-start(bf16[72,4096]{1,0:T(8,128)(2,1)S(1)} %get-tuple-element.88), channel_id=1, source_target_pairs={{0,16},{1,17},{2,18},{3,19},{4,20},{5,21},{6,22},{7,23},{8,24},{9,... | collective-permute-start | bytes 1769480 | tf_op jit(solution)/shard_map/ppermute | solution.py:328
  145.8 34.5 %collective-permute-start.36 = (bf16[40,4096]{1,0:T(8,128)(2,1)S(1)}, bf16[40,4096]{1,0:T(8,128)(2,1)S(1)}, u32[]{:S(2)}, u32[]{:S(2)}) collective-permute-start(bf16[40,4096]{1,0:T(8,128)(2,1)S(1)} %get-tuple-element.123), channel_id=1, source_target_pairs={{0,16},{1,17},{2,18},{3,19},{4,20},{5,21},{6,22},{7,23},{8,24},{9,... | collective-permute-start | bytes 983048 | tf_op jit(solution)/shard_map/ppermute | solution.py:328
  152.8 35.0 %collective-permute-start.37 = (bf16[40,4096]{1,0:T(8,128)(2,1)S(1)}, bf16[40,4096]{1,0:T(8,128)(2,1)S(1)}, u32[]{:S(2)}, u32[]{:S(2)}) collective-permute-start(bf16[40,4096]{1,0:T(8,128)(2,1)S(1)} %get-tuple-element.124), channel_id=1, source_target_pairs={{0,24},{1,25},{2,26},{3,27},{4,28},{5,29},{6,30},{7,31},{8,16},{9,... | collective-permute-start | bytes 983048 | tf_op jit(solution)/shard_map/ppermute | solution.py:328
  180.3 11.3 %collective-permute-start.3 = (bf16[40,4096]{1,0:T(8,128)(2,1)S(1)}, bf16[40,4096]{1,0:T(8,128)(2,1)S(1)}, u32[]{:S(2)}, u32[]{:S(2)}) collective-permute-start(bf16[40,4096]{1,0:T(8,128)(2,1)S(1)} %get-tuple-element.84), channel_id=1, source_target_pairs={{0,24},{1,25},{2,26},{3,27},{4,28},{5,29},{6,30},{7,31},{8,16},{9,... | collective-permute-start | bytes 983048 | tf_op jit(solution)/shard_map/ppermute | solution.py:328
  187.9 10.0 %collective-permute-start.30 = (bf16[72,2048]{1,0:T(8,128)(2,1)S(1)}, bf16[72,2048]{1,0:T(8,128)(2,1)S(1)}, u32[]{:S(2)}, u32[]{:S(2)}) collective-permute-start(bf16[72,2048]{1,0:T(8,128)(2,1)S(1)} %get-tuple-element.117), channel_id=1, source_target_pairs={{0,8},{1,9},{2,10},{3,11},{4,12},{5,13},{6,14},{7,15},{8,0},{9,1},... | collective-permute-start | bytes 884744 | tf_op jit(solution)/shard_map/ppermute | solution.py:328
  191.7 12.6 %collective-permute-start.38 = (bf16[40,2048]{1,0:T(8,128)(2,1)S(1)}, bf16[40,2048]{1,0:T(8,128)(2,1)S(1)}, u32[]{:S(2)}, u32[]{:S(2)}) collective-permute-start(bf16[40,2048]{1,0:T(8,128)(2,1)S(1)} %get-tuple-element.126), channel_id=1, source_target_pairs={{0,8},{1,9},{2,10},{3,11},{4,12},{5,13},{6,14},{7,15},{8,0},{9,1},... | collective-permute-start | bytes 491528 | tf_op jit(solution)/shard_map/ppermute | solution.py:328
  193.8 10.8 %collective-permute-start.39 = (bf16[40,2048]{1,0:T(8,128)(2,1)S(1)}, bf16[40,2048]{1,0:T(8,128)(2,1)S(1)}, u32[]{:S(2)}, u32[]{:S(2)}) collective-permute-start(bf16[40,2048]{1,0:T(8,128)(2,1)S(1)} %get-tuple-element.127), channel_id=1, source_target_pairs={{0,16},{1,17},{2,18},{3,19},{4,20},{5,21},{6,22},{7,23},{8,24},{9,... | collective-permute-start | bytes 491528 | tf_op jit(solution)/shard_map/ppermute | solution.py:328
  193.8 13.5 %collective-permute-start.40 = (bf16[40,2048]{1,0:T(8,128)(2,1)S(1)}, bf16[40,2048]{1,0:T(8,128)(2,1)S(1)}, u32[]{:S(2)}, u32[]{:S(2)}) collective-permute-start(bf16[40,2048]{1,0:T(8,128)(2,1)S(1)} %get-tuple-element.128), channel_id=1, source_target_pairs={{0,24},{1,25},{2,26},{3,27},{4,28},{5,29},{6,30},{7,31},{8,16},{9,... | collective-permute-start | bytes 491528 | tf_op jit(solution)/shard_map/ppermute | solution.py:328
  196.5 13.7 %collective-permute-start.31 = (bf16[72,2048]{1,0:T(8,128)(2,1)S(1)}, bf16[72,2048]{1,0:T(8,128)(2,1)S(1)}, u32[]{:S(2)}, u32[]{:S(2)}) collective-permute-start(bf16[72,2048]{1,0:T(8,128)(2,1)S(1)} %get-tuple-element.118), channel_id=1, source_target_pairs={{0,16},{1,17},{2,18},{3,19},{4,20},{5,21},{6,22},{7,23},{8,24},{9,... | collective-permute-start | bytes 884744 | tf_op jit(solution)/shard_map/ppermute | solution.py:328
  197.8 17.6 %collective-permute-start.32 = (bf16[72,2048]{1,0:T(8,128)(2,1)S(1)}, bf16[72,2048]{1,0:T(8,128)(2,1)S(1)}, u32[]{:S(2)}, u32[]{:S(2)}) collective-permute-start(bf16[72,2048]{1,0:T(8,128)(2,1)S(1)} %get-tuple-element.119), channel_id=1, source_target_pairs={{0,24},{1,25},{2,26},{3,27},{4,28},{5,29},{6,30},{7,31},{8,16},{9,... | collective-permute-start | bytes 884744 | tf_op jit(solution)/shard_map/ppermute | solution.py:328
  204.3 24.8 %collective-permute-start.16 = (bf16[72,4096]{1,0:T(8,128)(2,1)S(1)}, bf16[72,4096]{1,0:T(8,128)(2,1)S(1)}, u32[]{:S(2)}, u32[]{:S(2)}) collective-permute-start(bf16[72,4096]{1,0:T(8,128)(2,1)S(1)} %get-tuple-element.100), channel_id=1, source_target_pairs={{0,8},{1,9},{2,10},{3,11},{4,12},{5,13},{6,14},{7,15},{8,0},{9,1},... | collective-permute-start | bytes 1769480 | tf_op jit(solution)/shard_map/ppermute | solution.py:328
  204.5 27.0 %collective-permute-start.17 = (bf16[72,4096]{1,0:T(8,128)(2,1)S(1)}, bf16[72,4096]{1,0:T(8,128)(2,1)S(1)}, u32[]{:S(2)}, u32[]{:S(2)}) collective-permute-start(bf16[72,4096]{1,0:T(8,128)(2,1)S(1)} %get-tuple-element.101), channel_id=1, source_target_pairs={{0,16},{1,17},{2,18},{3,19},{4,20},{5,21},{6,22},{7,23},{8,24},{9,... | collective-permute-start | bytes 1769480 | tf_op jit(solution)/shard_map/ppermute | solution.py:328
  207.3 29.7 %collective-permute-start.18 = (bf16[72,4096]{1,0:T(8,128)(2,1)S(1)}, bf16[72,4096]{1,0:T(8,128)(2,1)S(1)}, u32[]{:S(2)}, u32[]{:S(2)}) collective-permute-start(bf16[72,4096]{1,0:T(8,128)(2,1)S(1)} %get-tuple-element.102), channel_id=1, source_target_pairs={{0,24},{1,25},{2,26},{3,27},{4,28},{5,29},{6,30},{7,31},{8,16},{9,... | collective-permute-start | bytes 1769480 | tf_op jit(solution)/shard_map/ppermute | solution.py:328
  210.2 15.9 %collective-permute-start.41 = (bf16[128,1024]{1,0:T(8,128)(2,1)S(1)}, bf16[128,1024]{1,0:T(8,128)(2,1)S(1)}, u32[]{:S(2)}, u32[]{:S(2)}) collective-permute-start(bf16[128,1024]{1,0:T(8,128)(2,1)S(1)} %get-tuple-element.129), channel_id=1, source_target_pairs={{0,1},{1,0},{2,3},{3,2},{4,5},{5,4},{6,7},{7,6},{8,9},{9,8},{10,11... | collective-permute-start | bytes 786440 | tf_op jit(solution)/shard_map/ppermute | solution.py:338
  215.4 10.8 %collective-permute-start.42 = (bf16[128,1024]{1,0:T(8,128)(2,1)S(1)}, bf16[128,1024]{1,0:T(8,128)(2,1)S(1)}, u32[]{:S(2)}, u32[]{:S(2)}) collective-permute-start(bf16[128,1024]{1,0:T(8,128)(2,1)S(1)} %get-tuple-element.130), channel_id=1, source_target_pairs={{0,7},{1,2},{2,1},{3,4},{4,3},{5,6},{6,5},{7,0},{8,15},{9,10},{10,... | collective-permute-start | bytes 786440 | tf_op jit(solution)/shard_map/ppermute | solution.py:338
  227.5 42.4 %collective-permute-start.43 = (bf16[128,2048]{1,0:T(8,128)(2,1)S(1)}, bf16[128,2048]{1,0:T(8,128)(2,1)S(1)}, u32[]{:S(2)}, u32[]{:S(2)}) collective-permute-start(bf16[128,2048]{1,0:T(8,128)(2,1)S(1)} %get-tuple-element.131), channel_id=1, source_target_pairs={{0,1},{1,0},{2,3},{3,2},{4,5},{5,4},{6,7},{7,6},{8,9},{9,8},{10,11... | collective-permute-start | bytes 1572872 | tf_op jit(solution)/shard_map/ppermute | solution.py:338
  227.6 42.3 %collective-permute-start.44 = (bf16[128,2048]{1,0:T(8,128)(2,1)S(1)}, bf16[128,2048]{1,0:T(8,128)(2,1)S(1)}, u32[]{:S(2)}, u32[]{:S(2)}) collective-permute-start(bf16[128,2048]{1,0:T(8,128)(2,1)S(1)} %get-tuple-element.132), channel_id=1, source_target_pairs={{0,7},{1,2},{2,1},{3,4},{4,3},{5,6},{6,5},{7,0},{8,15},{9,10},{10,... | collective-permute-start | bytes 1572872 | tf_op jit(solution)/shard_map/ppermute | solution.py:338
  241.7 8.9 %collective-permute-start.19 = (bf16[72,2048]{1,0:T(8,128)(2,1)S(1)}, bf16[72,2048]{1,0:T(8,128)(2,1)S(1)}, u32[]{:S(2)}, u32[]{:S(2)}) collective-permute-start(bf16[72,2048]{1,0:T(8,128)(2,1)S(1)} %get-tuple-element.104), channel_id=1, source_target_pairs={{0,8},{1,9},{2,10},{3,11},{4,12},{5,13},{6,14},{7,15},{8,0},{9,1},... | collective-permute-start | bytes 884744 | tf_op jit(solution)/shard_map/ppermute | solution.py:328
  242.0 13.5 %collective-permute-start.20 = (bf16[72,2048]{1,0:T(8,128)(2,1)S(1)}, bf16[72,2048]{1,0:T(8,128)(2,1)S(1)}, u32[]{:S(2)}, u32[]{:S(2)}) collective-permute-start(bf16[72,2048]{1,0:T(8,128)(2,1)S(1)} %get-tuple-element.105), channel_id=1, source_target_pairs={{0,16},{1,17},{2,18},{3,19},{4,20},{5,21},{6,22},{7,23},{8,24},{9,... | collective-permute-start | bytes 884744 | tf_op jit(solution)/shard_map/ppermute | solution.py:328
  245.2 24.7 %collective-permute-start.21 = (bf16[72,2048]{1,0:T(8,128)(2,1)S(1)}, bf16[72,2048]{1,0:T(8,128)(2,1)S(1)}, u32[]{:S(2)}, u32[]{:S(2)}) collective-permute-start(bf16[72,2048]{1,0:T(8,128)(2,1)S(1)} %get-tuple-element.106), channel_id=1, source_target_pairs={{0,24},{1,25},{2,26},{3,27},{4,28},{5,29},{6,30},{7,31},{8,16},{9,... | collective-permute-start | bytes 884744 | tf_op jit(solution)/shard_map/ppermute | solution.py:328
  250.7 26.9 %collective-permute-start.13 = (bf16[112,2048]{1,0:T(8,128)(2,1)S(1)}, bf16[112,2048]{1,0:T(8,128)(2,1)S(1)}, u32[]{:S(2)}, u32[]{:S(2)}) collective-permute-start(bf16[112,2048]{1,0:T(8,128)(2,1)S(1)} %pad_maximum_fusion.6), channel_id=1, source_target_pairs={{0,24},{1,25},{2,26},{3,27},{4,28},{5,29},{6,30},{7,31},{8,16},{9,... | collective-permute-start | bytes 1376264 | tf_op jit(solution)/shard_map/ppermute | solution.py:328
  255.5 22.1 %collective-permute-start.12 = (bf16[112,2048]{1,0:T(8,128)(2,1)S(1)}, bf16[112,2048]{1,0:T(8,128)(2,1)S(1)}, u32[]{:S(2)}, u32[]{:S(2)}) collective-permute-start(bf16[112,2048]{1,0:T(8,128)(2,1)S(1)} %pad_maximum_fusion.5), channel_id=1, source_target_pairs={{0,16},{1,17},{2,18},{3,19},{4,20},{5,21},{6,22},{7,23},{8,24},{9,... | collective-permute-start | bytes 1376264 | tf_op jit(solution)/shard_map/ppermute | solution.py:328
  270.9 11.4 %collective-permute-start.45 = (bf16[128,2048]{1,0:T(8,128)(2,1)S(1)}, bf16[128,2048]{1,0:T(8,128)(2,1)S(1)}, u32[]{:S(2)}, u32[]{:S(2)}) collective-permute-start(bf16[128,2048]{1,0:T(8,128)(2,1)S(1)} %get-tuple-element.133), channel_id=1, source_target_pairs={{0,1},{1,0},{2,3},{3,2},{4,5},{5,4},{6,7},{7,6},{8,9},{9,8},{10,11... | collective-permute-start | bytes 1572872 | tf_op jit(solution)/shard_map/ppermute | solution.py:338
  271.4 10.8 %collective-permute-start.46 = (bf16[128,2048]{1,0:T(8,128)(2,1)S(1)}, bf16[128,2048]{1,0:T(8,128)(2,1)S(1)}, u32[]{:S(2)}, u32[]{:S(2)}) collective-permute-start(bf16[128,2048]{1,0:T(8,128)(2,1)S(1)} %get-tuple-element.134), channel_id=1, source_target_pairs={{0,7},{1,2},{2,1},{3,4},{4,3},{5,6},{6,5},{7,0},{8,15},{9,10},{10,... | collective-permute-start | bytes 1572872 | tf_op jit(solution)/shard_map/ppermute | solution.py:338
  283.2 20.5 %collective-permute-start.47 = (bf16[128,2048]{1,0:T(8,128)(2,1)S(1)}, bf16[128,2048]{1,0:T(8,128)(2,1)S(1)}, u32[]{:S(2)}, u32[]{:S(2)}) collective-permute-start(bf16[128,2048]{1,0:T(8,128)(2,1)S(1)} %get-tuple-element.135), channel_id=1, source_target_pairs={{0,1},{1,0},{2,3},{3,2},{4,5},{5,4},{6,7},{7,6},{8,9},{9,8},{10,11... | collective-permute-start | bytes 1572872 | tf_op jit(solution)/shard_map/ppermute | solution.py:338
  283.8 19.9 %collective-permute-start.48 = (bf16[128,2048]{1,0:T(8,128)(2,1)S(1)}, bf16[128,2048]{1,0:T(8,128)(2,1)S(1)}, u32[]{:S(2)}, u32[]{:S(2)}) collective-permute-start(bf16[128,2048]{1,0:T(8,128)(2,1)S(1)} %get-tuple-element.136), channel_id=1, source_target_pairs={{0,7},{1,2},{2,1},{3,4},{4,3},{5,6},{6,5},{7,0},{8,15},{9,10},{10,... | collective-permute-start | bytes 1572872 | tf_op jit(solution)/shard_map/ppermute | solution.py:338
  (7 other events, 165.5 us)
